TPU v7x, 32 devices: a whole 2x2x4 slice. The times are simulated.
32 devices in a mesh: dp: 8 (over y, x, core), tensor: 4 (over z).
Axes of the slice: x: 2, y: 2, z: 4, core: 2. Of those that a mesh axis runs over, the one named last changes fastest.
Arguments:
- inputs: bfloat16 [2, 1024, 1024], P(None, ('dp', 'tensor')), may hold values from -6 to 6
- out_grad: bfloat16 [2, 1024, 1024], P(None, ('dp', 'tensor')), may hold values from -6 to 6
- saved: bfloat16 [2, 1024, 32768], P(None, 'dp', 'tensor'), may hold values from 0 to 16, as said below
- w_in: bfloat16 [1024, 32768], P(None, 'tensor'), may hold values from -0.1875 to 0.1875
- w_out: bfloat16 [1024, 32768], P(None, 'tensor'), may hold values from -0.03125 to 0.03125
- mom_in: float32 [1024, 32768], P('dp', 'tensor'), may hold values from -3 to 3
Outputs:
- in_grad: float32 [2, 1024, 1024], P(None, ('dp', 'tensor'))
- new_mom_in: float32 [1024, 32768], P('dp', 'tensor')
Inputs may be any that keep to these rules, and one draw needn't show every extreme that they name: `saved`: every entry is zero or positive.
All inputs are finite; a program needn't handle non-finite values.
Results may differ from a plain program's by a relative error of at most 0.0029.
Values may be sent and summed in bfloat16 or wider, within the bound.
A program may use at most 128 MiB of HBM per device.

v0:
```python
import jax
import jax.numpy as jnp
from jax import lax
from jax.sharding import PartitionSpec as P


momentum_decay = 0.9
PIECES = 2
SMALL_AXIS = 8


def xor_send(value, size, mask):
    return lax.ppermute(value, "dp", [(i, i ^ mask) for i in range(size)])


def gather_rows(value):
    size = lax.axis_size("tensor")
    if size > SMALL_AXIS:
        return lax.all_gather(value, "tensor", axis=1, tiled=True)
    me = lax.axis_index("tensor")
    rows = value.shape[1]
    shape = (value.shape[0], rows * size) + value.shape[2:]
    moved = [value] + [
        lax.ppermute(value, "tensor", [(i, (i + k) % size) for i in range(size)])
        for k in range(1, size)
    ]
    full = jnp.zeros(shape, value.dtype)
    for k, piece in enumerate(moved):
        start = (me - k + size) % size * rows
        full = lax.dynamic_update_slice_in_dim(full, piece, start, axis=1)
    return full


def scatter_rows(terms):
    size = lax.axis_size("tensor")
    if size > SMALL_AXIS:
        return lax.psum_scatter(terms, "tensor", scatter_dimension=1, tiled=True)
    me = lax.axis_index("tensor")
    rows = terms.shape[1] // size
    total = lax.dynamic_slice_in_dim(terms, me * rows, rows, axis=1)
    for k in range(1, size):
        start = (me + k) % size * rows
        piece = lax.dynamic_slice_in_dim(terms, start, rows, axis=1).astype(jnp.bfloat16)
        got = lax.ppermute(piece, "tensor", [(i, (i + k) % size) for i in range(size)])
        total = total + got.astype(jnp.float32)
    return total


def spans(bits):
    masks = [0]
    for bit in bits:
        masks = masks + [m | bit for m in masks]
    return masks


def transpose_dot(left_rows, right_rows):
    return lax.dot_general(
        left_rows, right_rows, (((0,), (0,)), ((), ())), preferred_element_type=jnp.float32
    )


def step_body(inputs, out_grad, saved, w_in, w_out, mom_in):
    micro_count, _, model_width = inputs.shape
    hidden_width = saved.shape[2]
    size = lax.axis_size("dp")
    me = lax.axis_index("dp")
    own_rows = model_width // size
    bits = [1 << b for b in range(1, size.bit_length() - 1)]
    orders = [(bits[0], bits[1:]), (bits[-1], bits[:-1])]

    def columns_of(owner, masks):
        return jnp.concatenate(
            [
                lax.dynamic_slice_in_dim(inputs, (owner ^ m) * own_rows, own_rows, axis=2)
                for m in masks
            ],
            axis=2,
        )

    grad_rows = gather_rows(out_grad).reshape(-1, model_width)

    pieces = []
    for first, rest in orders:
        masks = spans(rest)
        pieces.append(columns_of(me, masks))
        for m in (1, first, first | 1):
            pieces.append(xor_send(columns_of(me ^ m, masks), size, m))
    packed = jnp.concatenate(pieces, axis=2)
    packed, grad_rows = lax.optimization_barrier((packed, grad_rows))
    packed = gather_rows(packed)
    packed = packed.reshape(-1, packed.shape[2])
    width = packed.shape[1] // (4 * len(orders))

    saved_rows = saved.reshape(-1, hidden_width)
    half = hidden_width // len(orders)
    step = half // PIECES
    chunks = [(o, o * half + p * step) for p in range(PIECES) for o in range(len(orders))]

    hidden, near, pair = [], [], []
    for c, (o, start) in enumerate(chunks):
        product = jnp.dot(
            grad_rows, w_out[:, start:start + step], preferred_element_type=jnp.float32
        )
        mask = saved_rows[:, start:start + step] > 0
        hidden.append(jnp.where(mask, product, 0.0).astype(jnp.bfloat16))
        near.append(xor_send(hidden[c], size, orders[o][0]))
        pair.append(xor_send(hidden[c], size, 1))

    ordered = [hidden[c] for c in sorted(range(len(chunks)), key=lambda c: chunks[c][1])]
    input_terms = lax.dot_general(
        jnp.concatenate(ordered, axis=1), w_in, (((1,), (1,)), ((), ())),
        preferred_element_type=jnp.float32,
    ).reshape(micro_count, -1, model_width)
    in_grad = scatter_rows(input_terms)

    new_mom_in = momentum_decay * mom_in
    arrived = []
    for c, (o, start) in enumerate(chunks):
        first, rest = orders[o]
        tokens = packed[:, o * 4 * width:(o + 1) * 4 * width]
        terms = [tokens[:, i * width:(i + 1) * width] for i in range(4)]
        early = transpose_dot(terms[0], hidden[c]) + transpose_dot(terms[1], pair[c])
        early = lax.optimization_barrier(early)
        near_pair = xor_send(near[c], size, 1)
        total = early + transpose_dot(terms[2], near[c])
        total = total + transpose_dot(terms[3], near_pair)
        kept = total[:own_rows]
        for i, m in enumerate(spans(rest)):
            if m:
                part = total[i * own_rows:(i + 1) * own_rows].astype(jnp.bfloat16)
                arrived.append((c, xor_send(part, size, m)))
        old = new_mom_in[:, start:start + step]
        new_mom_in = new_mom_in.at[:, start:start + step].set(old + kept / size)
    for c, part in arrived:
        start = chunks[c][1]
        old = new_mom_in[:, start:start + step]
        update = old + part.astype(jnp.float32) / size
        new_mom_in = new_mom_in.at[:, start:start + step].set(update)
    return (in_grad, new_mom_in)


def solution(mesh):
    placed = (
        P(None, ("dp", "tensor"), None),
        P(None, ("dp", "tensor"), None),
        P(None, "dp", "tensor"),
        P(None, "tensor"),
        P(None, "tensor"),
        P("dp", "tensor"),
    )
    return jax.shard_map(
        step_body,
        mesh=mesh,
        in_specs=placed,
        out_specs=(P(None, ("dp", "tensor"), None), P("dp", "tensor")),
        check_vma=False,
    )
```

profile of v0, /device:TPU:24, one launch (start us, length us, event | category | flops | bytes accessed | tf_op | source)
XLA Modules:
  0.0 164.7 jit_solution(5353401727194795877)
XLA Ops:
  0.7 1.9 %collective-permute-start.7 = (bf16[2,32,1024]{2,1,0:T(8,128)(2,1)}, bf16[2,32,1024]{2,1,0:T(8,128)(2,1)S(1)}, u32[]{:S(2)}, u32[]{:S(2)}) collective-permute-start(bf16[2,32,1024]{2,1,0:T(8,128)(2,1)} %param.23), channel_id=1, source_target_pairs={{0,2},{1,3},{2,0},{3,1},{4,6},{5,7},{6,4},{7,5},{8,10},{9,11},{10,... | collective-permute-start | bytes 393224 | tf_op jit(solution)/shard_map/ppermute | solution.py:24
  4.0 1.6 collective-permute-start.1
  5.6 4.7 %broadcast_multiply_fusion = f32[128,8192]{1,0:T(8,128)} fusion(f32[128,8192]{1,0:T(8,128)} %param.27), kind=kLoop, calls=%fused_computation.36 | loop fusion | flops 1048576 | bytes 8388608 | tf_op jit(solution)/shard_map/mul | solution.py:116
  13.9 2.7 %collective-permute-done.2 = bf16[2,32,256]{2,1,0:T(8,128)(2,1)S(1)} collective-permute-done((bf16[2,32,256]{2,1,0:T(8,128)(2,1)S(1)}, bf16[2,32,256]{2,1,0:T(8,128)(2,1)S(1)}, u32[]{:S(2)}, u32[]{:S(2)}) %collective-permute-start.2) | collective-permute-done | bytes 32800 | tf_op jit(solution)/shard_map/ppermute | solution.py:13
  16.6 1.5 collective-permute-start.4
  18.9 1.5 collective-permute-done.4
  20.5 2.1 %collective-permute-done.5 = bf16[2,32,256]{2,1,0:T(8,128)(2,1)S(1)} collective-permute-done((bf16[2,32,256]{2,1,0:T(8,128)(2,1)S(1)}, bf16[2,32,256]{2,1,0:T(8,128)(2,1)S(1)}, u32[]{:S(2)}, u32[]{:S(2)}) %collective-permute-start.5) | collective-permute-done | bytes 32800 | tf_op jit(solution)/shard_map/ppermute | solution.py:13
  22.7 3.9 %fusion.37 = bf16[256,2048]{1,0:T(8,128)(2,1)S(1)} fusion(bf16[256,1024]{1,0:T(8,128)(2,1)S(1)} %bitcast.41, bf16[1024,8192]{1,0:T(8,128)(2,1)} %param.26, bf16[256,8192]{1,0:T(8,128)(2,1)} %bitcast.47), kind=kOutput, calls=%fused_computation.35 | convolution fusion | flops 1075314688 | bytes 6815744 | tf_op jit(solution)/shard_map/dot_general | solution.py:101
  26.6 3.5 %fusion.31 = bf16[256,2048]{1,0:T(8,128)(2,1)S(1)} fusion(bf16[256,1024]{1,0:T(8,128)(2,1)S(1)} %bitcast.42, bf16[1024,8192]{1,0:T(8,128)(2,1)} %param.26, bf16[256,8192]{1,0:T(8,128)(2,1)S(1)} %bitcast.48), kind=kOutput, calls=%fused_computation.33 | convolution fusion | flops 1075314688 | bytes 6815744 | tf_op jit(solution)/shard_map/dot_general | solution.py:101
  30.1 3.5 %fusion.25 = bf16[256,2048]{1,0:T(8,128)(2,1)S(1)} fusion(bf16[256,1024]{1,0:T(8,128)(2,1)S(1)} %bitcast.43, bf16[1024,8192]{1,0:T(8,128)(2,1)} %param.26, bf16[256,8192]{1,0:T(8,128)(2,1)S(1)} %bitcast.49), kind=kOutput, calls=%fused_computation.31 | convolution fusion | flops 1075314688 | bytes 6815744 | tf_op jit(solution)/shard_map/dot_general | solution.py:101
  33.6 3.5 %fusion.19 = bf16[256,2048]{1,0:T(8,128)(2,1)S(1)} fusion(bf16[256,1024]{1,0:T(8,128)(2,1)S(1)} %bitcast.44, bf16[1024,8192]{1,0:T(8,128)(2,1)} %param.26, bf16[256,8192]{1,0:T(8,128)(2,1)S(1)} %bitcast.50), kind=kOutput, calls=%fused_computation.29 | convolution fusion | flops 1075314688 | bytes 6815744 | tf_op jit(solution)/shard_map/dot_general | solution.py:101
  37.3 10.3 %fusion = f32[256,1024]{1,0:T(8,128)S(1)} fusion(bf16[1024,8192]{1,0:T(8,128)(2,1)} %param.25, bf16[256,2048]{1,0:T(8,128)(2,1)S(1)} %fusion.37, bf16[256,2048]{1,0:T(8,128)(2,1)S(1)} %fusion.31, bf16[256,2048]{1,0:T(8,128)(2,1)S(1)} %fusion.25, bf16[256,2048]{1,0:T(8,128)(2,1)S(1)} %fusion.19), kind=kOutput, calls=%fused_computation | convolution fusion | flops 4311744512 | bytes 22020096 | tf_op jit(solution)/shard_map/dot_general | solution.py:110
  47.6 1.4 collective-permute-start.11
  49.0 2.6 %collective-permute-start.10 = (bf16[2,32,1024]{2,1,0:T(8,128)(2,1)S(1)}, bf16[2,32,1024]{2,1,0:T(8,128)(2,1)S(1)}, u32[]{:S(2)}, u32[]{:S(2)}) collective-permute-start(bf16[2,32,1024]{2,1,0:T(8,128)(2,1)S(1)} %get-tuple-element.106), channel_id=1, source_target_pairs={{0,2},{1,3},{2,0},{3,1},{4,6},{5,7},{6,4},{7,5},{8,10},{9,11},{10,... | collective-permute-start | bytes 393224 | tf_op jit(solution)/shard_map/ppermute | solution.py:44
  51.6 1.6 collective-permute-start.9
  53.6 2.4 %collective-permute-done.11 = bf16[2,32,1024]{2,1,0:T(8,128)(2,1)S(1)} collective-permute-done((bf16[2,32,1024]{2,1,0:T(8,128)(2,1)S(1)}, bf16[2,32,1024]{2,1,0:T(8,128)(2,1)S(1)}, u32[]{:S(2)}, u32[]{:S(2)}) %collective-permute-start.11) | collective-permute-done | bytes 131104 | tf_op jit(solution)/shard_map/ppermute | solution.py:44
  56.0 14.7 %collective-permute-start.13 = (bf16[2,32,2048]{2,1,0:T(8,128)(2,1)S(1)}, bf16[2,32,2048]{2,1,0:T(8,128)(2,1)S(1)}, u32[]{:S(2)}, u32[]{:S(2)}) collective-permute-start(bf16[2,32,2048]{2,1,0:T(8,128)(2,1)S(1)} %constant_dynamic-update-slice_fusion), channel_id=1, source_target_pairs={{0,2},{1,3},{2,0},{3,1},{4,6},{5,7},{6,4},{7,5},{8,10},{9,11},{10,... | collective-permute-start | bytes 786440 | tf_op jit(solution)/shard_map/ppermute | solution.py:24
  72.9 13.3 %collective-permute-done.13 = bf16[2,32,2048]{2,1,0:T(8,128)(2,1)S(1)} collective-permute-done((bf16[2,32,2048]{2,1,0:T(8,128)(2,1)S(1)}, bf16[2,32,2048]{2,1,0:T(8,128)(2,1)S(1)}, u32[]{:S(2)}, u32[]{:S(2)}) %collective-permute-start.13) | collective-permute-done | bytes 262176 | tf_op jit(solution)/shard_map/ppermute | solution.py:24
  89.6 1.6 collective-permute-start.25
  93.2 4.4 %collective-permute-done.16 = bf16[256,2048]{1,0:T(8,128)(2,1)S(1)} collective-permute-done((bf16[256,2048]{1,0:T(8,128)(2,1)S(1)}, bf16[256,2048]{1,0:T(8,128)(2,1)S(1)}, u32[]{:S(2)}, u32[]{:S(2)}) %collective-permute-start.16) | collective-permute-done | bytes 1048608 | tf_op jit(solution)/shard_map/ppermute | solution.py:13
  97.6 14.6 %collective-permute-done.19 = bf16[256,2048]{1,0:T(8,128)(2,1)S(1)} collective-permute-done((bf16[256,2048]{1,0:T(8,128)(2,1)S(1)}, bf16[256,2048]{1,0:T(8,128)(2,1)S(1)}, u32[]{:S(2)}, u32[]{:S(2)}) %collective-permute-start.19) | collective-permute-done | bytes 1048608 | tf_op jit(solution)/shard_map/ppermute | solution.py:13
  112.3 5.5 %collective-permute-done.22 = bf16[256,2048]{1,0:T(8,128)(2,1)S(1)} collective-permute-done((bf16[256,2048]{1,0:T(8,128)(2,1)S(1)}, bf16[256,2048]{1,0:T(8,128)(2,1)S(1)}, u32[]{:S(2)}, u32[]{:S(2)}) %collective-permute-start.22) | collective-permute-done | bytes 1048608 | tf_op jit(solution)/shard_map/ppermute | solution.py:13
  118.3 15.5 %collective-permute-done.25 = bf16[256,2048]{1,0:T(8,128)(2,1)S(1)} collective-permute-done((bf16[256,2048]{1,0:T(8,128)(2,1)S(1)}, bf16[256,2048]{1,0:T(8,128)(2,1)S(1)}, u32[]{:S(2)}, u32[]{:S(2)}) %collective-permute-start.25) | collective-permute-done | bytes 1048608 | tf_op jit(solution)/shard_map/ppermute | solution.py:13
  137.9 1.0 fusion.40
  139.4 1.1 fusion.41
  142.4 1.1 collective-permute-start.29
  143.5 1.5 collective-permute-start.30
  145.0 5.6 %collective-permute-done.27 = bf16[128,2048]{1,0:T(8,128)(2,1)S(1)} collective-permute-done((bf16[128,2048]{1,0:T(8,128)(2,1)S(1)}, bf16[128,2048]{1,0:T(8,128)(2,1)S(1)}, u32[]{:S(2)}, u32[]{:S(2)}) %collective-permute-start.27) | collective-permute-done | bytes 524320 | tf_op jit(solution)/shard_map/ppermute | solution.py:13
  150.6 1.0 fusion.43
  151.7 1.1 fusion.44
  152.8 8.6 %collective-permute-done.29 = bf16[128,2048]{1,0:T(8,128)(2,1)S(1)} collective-permute-done((bf16[128,2048]{1,0:T(8,128)(2,1)S(1)}, bf16[128,2048]{1,0:T(8,128)(2,1)S(1)}, u32[]{:S(2)}, u32[]{:S(2)}) %collective-permute-start.29) | collective-permute-done | bytes 524320 | tf_op jit(solution)/shard_map/ppermute | solution.py:13
  162.7 2.0 %copy-done.1 = f32[128,8192]{1,0:T(8,128)} copy-done((f32[128,8192]{1,0:T(8,128)}, f32[128,8192]{1,0:T(8,128)S(1)}, u32[]{:S(2)}) %copy-start.1) | copy-done | bytes 4194328
  (102 shorter events, 22.1 us)
Async XLA Ops:
  0.6 21.9 %collective-permute-start.6 = (bf16[2,32,1024]{2,1,0:T(8,128)(2,1)}, bf16[2,32,1024]{2,1,0:T(8,128)(2,1)S(1)}, u32[]{:S(2)}, u32[]{:S(2)}) collective-permute-start(bf16[2,32,1024]{2,1,0:T(8,128)(2,1)} %param.23), channel_id=1, source_target_pairs={{0,1},{1,2},{2,3},{3,0},{4,5},{5,6},{6,7},{7,4},{8,9},{9,10},{10,1... | collective-permute-start | bytes 393224 | tf_op jit(solution)/shard_map/ppermute | solution.py:24
  0.7 21.9 %collective-permute-start.7 = (bf16[2,32,1024]{2,1,0:T(8,128)(2,1)}, bf16[2,32,1024]{2,1,0:T(8,128)(2,1)S(1)}, u32[]{:S(2)}, u32[]{:S(2)}) collective-permute-start(bf16[2,32,1024]{2,1,0:T(8,128)(2,1)} %param.23), channel_id=1, source_target_pairs={{0,2},{1,3},{2,0},{3,1},{4,6},{5,7},{6,4},{7,5},{8,10},{9,11},{10,... | collective-permute-start | bytes 393224 | tf_op jit(solution)/shard_map/ppermute | solution.py:24
  2.6 20.0 %collective-permute-start.8 = (bf16[2,32,1024]{2,1,0:T(8,128)(2,1)}, bf16[2,32,1024]{2,1,0:T(8,128)(2,1)S(1)}, u32[]{:S(2)}, u32[]{:S(2)}) collective-permute-start(bf16[2,32,1024]{2,1,0:T(8,128)(2,1)} %param.23), channel_id=1, source_target_pairs={{0,3},{1,0},{2,1},{3,2},{4,7},{5,4},{6,5},{7,6},{8,11},{9,8},{10,9... | collective-permute-start | bytes 393224 | tf_op jit(solution)/shard_map/ppermute | solution.py:24
  4.0 9.3 %collective-permute-start = (bf16[2,32,256]{2,1,0:T(8,128)(2,1)S(1)}, bf16[2,32,256]{2,1,0:T(8,128)(2,1)S(1)}, u32[]{:S(2)}, u32[]{:S(2)}) collective-permute-start(bf16[2,32,256]{2,1,0:T(8,128)(2,1)S(1)} %get-tuple-element.119), channel_id=1, source_target_pairs={{0,4},{4,0},{8,12},{12,8},{16,20},{20,16},{24,28},{28,24},{1,5},{5... | collective-permute-start | bytes 98312 | tf_op jit(solution)/shard_map/ppermute | solution.py:13
  4.0 9.5 %collective-permute-start.1 = (bf16[2,32,256]{2,1,0:T(8,128)(2,1)S(1)}, bf16[2,32,256]{2,1,0:T(8,128)(2,1)S(1)}, u32[]{:S(2)}, u32[]{:S(2)}) collective-permute-start(bf16[2,32,256]{2,1,0:T(8,128)(2,1)S(1)} %pad_maximum_fusion.2), channel_id=1, source_target_pairs={{0,8},{4,12},{8,0},{12,4},{16,24},{20,28},{24,16},{28,20},{1,9},{5... | collective-permute-start | bytes 98312 | tf_op jit(solution)/shard_map/ppermute | solution.py:13
  5.6 5.5 %copy-start.2 = (bf16[2,32,1024]{2,1,0:T(8,128)(2,1)S(1)}, bf16[2,32,1024]{2,1,0:T(8,128)(2,1)}, u32[]{:S(2)}) copy-start(bf16[2,32,1024]{2,1,0:T(8,128)(2,1)} %param.23) | copy-start | bytes 393220
  13.2 3.4 %collective-permute-start.2 = (bf16[2,32,256]{2,1,0:T(8,128)(2,1)S(1)}, bf16[2,32,256]{2,1,0:T(8,128)(2,1)S(1)}, u32[]{:S(2)}, u32[]{:S(2)}) collective-permute-start(bf16[2,32,256]{2,1,0:T(8,128)(2,1)S(1)} %pad_maximum_fusion.3), channel_id=1, source_target_pairs={{0,12},{4,8},{8,4},{12,0},{16,28},{20,24},{24,20},{28,16},{1,13},{... | collective-permute-start | bytes 98312 | tf_op jit(solution)/shard_map/ppermute | solution.py:13
  13.5 5.3 %collective-permute-start.3 = (bf16[2,32,256]{2,1,0:T(8,128)(2,1)S(1)}, bf16[2,32,256]{2,1,0:T(8,128)(2,1)S(1)}, u32[]{:S(2)}, u32[]{:S(2)}) collective-permute-start(bf16[2,32,256]{2,1,0:T(8,128)(2,1)S(1)} %get-tuple-element.118), channel_id=1, source_target_pairs={{0,4},{4,0},{8,12},{12,8},{16,20},{20,16},{24,28},{28,24},{1,5},{5... | collective-permute-start | bytes 98312 | tf_op jit(solution)/shard_map/ppermute | solution.py:13
  16.6 3.9 %collective-permute-start.4 = (bf16[2,32,256]{2,1,0:T(8,128)(2,1)S(1)}, bf16[2,32,256]{2,1,0:T(8,128)(2,1)S(1)}, u32[]{:S(2)}, u32[]{:S(2)}) collective-permute-start(bf16[2,32,256]{2,1,0:T(8,128)(2,1)S(1)} %pad_maximum_fusion.4), channel_id=1, source_target_pairs={{0,16},{4,20},{8,24},{12,28},{16,0},{20,4},{24,8},{28,12},{1,17},{... | collective-permute-start | bytes 98312 | tf_op jit(solution)/shard_map/ppermute | solution.py:13
  18.8 3.7 %collective-permute-start.5 = (bf16[2,32,256]{2,1,0:T(8,128)(2,1)S(1)}, bf16[2,32,256]{2,1,0:T(8,128)(2,1)S(1)}, u32[]{:S(2)}, u32[]{:S(2)}) collective-permute-start(bf16[2,32,256]{2,1,0:T(8,128)(2,1)S(1)} %pad_maximum_fusion.5), channel_id=1, source_target_pairs={{0,20},{4,16},{8,28},{12,24},{16,4},{20,0},{24,12},{28,8},{1,21},{... | collective-permute-start | bytes 98312 | tf_op jit(solution)/shard_map/ppermute | solution.py:13
  37.1 49.7 %collective-permute-start.15 = (bf16[256,2048]{1,0:T(8,128)(2,1)S(1)}, bf16[256,2048]{1,0:T(8,128)(2,1)S(1)}, u32[]{:S(2)}, u32[]{:S(2)}) collective-permute-start(bf16[256,2048]{1,0:T(8,128)(2,1)S(1)} %fusion.19), channel_id=1, source_target_pairs={{0,4},{4,0},{8,12},{12,8},{16,20},{20,16},{24,28},{28,24},{1,5},{5... | collective-permute-start | bytes 3145736 | tf_op jit(solution)/shard_map/ppermute | solution.py:13
  47.6 8.3 %collective-permute-start.11 = (bf16[2,32,1024]{2,1,0:T(8,128)(2,1)S(1)}, bf16[2,32,1024]{2,1,0:T(8,128)(2,1)S(1)}, u32[]{:S(2)}, u32[]{:S(2)}) collective-permute-start(bf16[2,32,1024]{2,1,0:T(8,128)(2,1)S(1)} %get-tuple-element.105), channel_id=1, source_target_pairs={{0,3},{1,0},{2,1},{3,2},{4,7},{5,4},{6,5},{7,6},{8,11},{9,8},{10,9... | collective-permute-start | bytes 393224 | tf_op jit(solution)/shard_map/ppermute | solution.py:44
  49.0 21.7 %collective-permute-start.10 = (bf16[2,32,1024]{2,1,0:T(8,128)(2,1)S(1)}, bf16[2,32,1024]{2,1,0:T(8,128)(2,1)S(1)}, u32[]{:S(2)}, u32[]{:S(2)}) collective-permute-start(bf16[2,32,1024]{2,1,0:T(8,128)(2,1)S(1)} %get-tuple-element.106), channel_id=1, source_target_pairs={{0,2},{1,3},{2,0},{3,1},{4,6},{5,7},{6,4},{7,5},{8,10},{9,11},{10,... | collective-permute-start | bytes 393224 | tf_op jit(solution)/shard_map/ppermute | solution.py:44
  51.6 20.0 %collective-permute-start.9 = (bf16[2,32,1024]{2,1,0:T(8,128)(2,1)S(1)}, bf16[2,32,1024]{2,1,0:T(8,128)(2,1)S(1)}, u32[]{:S(2)}, u32[]{:S(2)}) collective-permute-start(bf16[2,32,1024]{2,1,0:T(8,128)(2,1)S(1)} %get-tuple-element.104), channel_id=1, source_target_pairs={{0,1},{1,2},{2,3},{3,0},{4,5},{5,6},{6,7},{7,4},{8,9},{9,10},{10,1... | collective-permute-start | bytes 393224 | tf_op jit(solution)/shard_map/ppermute | solution.py:44
  53.2 19.7 %collective-permute-start.12 = (bf16[2,32,2048]{2,1,0:T(8,128)(2,1)S(1)}, bf16[2,32,2048]{2,1,0:T(8,128)(2,1)S(1)}, u32[]{:S(2)}, u32[]{:S(2)}) collective-permute-start(bf16[2,32,2048]{2,1,0:T(8,128)(2,1)S(1)} %constant_dynamic-update-slice_fusion), channel_id=1, source_target_pairs={{0,1},{1,2},{2,3},{3,0},{4,5},{5,6},{6,7},{7,4},{8,9},{9,10},{10,1... | collective-permute-start | bytes 786440 | tf_op jit(solution)/shard_map/ppermute | solution.py:24
  56.0 30.3 %collective-permute-start.13 = (bf16[2,32,2048]{2,1,0:T(8,128)(2,1)S(1)}, bf16[2,32,2048]{2,1,0:T(8,128)(2,1)S(1)}, u32[]{:S(2)}, u32[]{:S(2)}) collective-permute-start(bf16[2,32,2048]{2,1,0:T(8,128)(2,1)S(1)} %constant_dynamic-update-slice_fusion), channel_id=1, source_target_pairs={{0,2},{1,3},{2,0},{3,1},{4,6},{5,7},{6,4},{7,5},{8,10},{9,11},{10,... | collective-permute-start | bytes 786440 | tf_op jit(solution)/shard_map/ppermute | solution.py:24
  70.7 16.0 %collective-permute-start.14 = (bf16[2,32,2048]{2,1,0:T(8,128)(2,1)S(1)}, bf16[2,32,2048]{2,1,0:T(8,128)(2,1)S(1)}, u32[]{:S(2)}, u32[]{:S(2)}) collective-permute-start(bf16[2,32,2048]{2,1,0:T(8,128)(2,1)S(1)} %constant_dynamic-update-slice_fusion), channel_id=1, source_target_pairs={{0,3},{1,0},{2,1},{3,2},{4,7},{5,4},{6,5},{7,6},{8,11},{9,8},{10,9... | collective-permute-start | bytes 786440 | tf_op jit(solution)/shard_map/ppermute | solution.py:24
  71.6 26.0 %collective-permute-start.16 = (bf16[256,2048]{1,0:T(8,128)(2,1)S(1)}, bf16[256,2048]{1,0:T(8,128)(2,1)S(1)}, u32[]{:S(2)}, u32[]{:S(2)}) collective-permute-start(bf16[256,2048]{1,0:T(8,128)(2,1)S(1)} %fusion.19), channel_id=1, source_target_pairs={{0,8},{4,12},{8,0},{12,4},{16,24},{20,28},{24,16},{28,20},{1,9},{5... | collective-permute-start | bytes 3145736 | tf_op jit(solution)/shard_map/ppermute | solution.py:13
  72.9 15.5 %collective-permute-start.18 = (bf16[256,2048]{1,0:T(8,128)(2,1)S(1)}, bf16[256,2048]{1,0:T(8,128)(2,1)S(1)}, u32[]{:S(2)}, u32[]{:S(2)}) collective-permute-start(bf16[256,2048]{1,0:T(8,128)(2,1)S(1)} %fusion.31), channel_id=1, source_target_pairs={{0,4},{4,0},{8,12},{12,8},{16,20},{20,16},{24,28},{28,24},{1,5},{5... | collective-permute-start | bytes 3145736 | tf_op jit(solution)/shard_map/ppermute | solution.py:13
  86.2 26.0 %collective-permute-start.19 = (bf16[256,2048]{1,0:T(8,128)(2,1)S(1)}, bf16[256,2048]{1,0:T(8,128)(2,1)S(1)}, u32[]{:S(2)}, u32[]{:S(2)}) collective-permute-start(bf16[256,2048]{1,0:T(8,128)(2,1)S(1)} %fusion.31), channel_id=1, source_target_pairs={{0,16},{4,20},{8,24},{12,28},{16,0},{20,4},{24,8},{28,12},{1,17},{... | collective-permute-start | bytes 3145736 | tf_op jit(solution)/shard_map/ppermute | solution.py:13
  86.7 2.9 %collective-permute-start.21 = (bf16[256,2048]{1,0:T(8,128)(2,1)S(1)}, bf16[256,2048]{1,0:T(8,128)(2,1)S(1)}, u32[]{:S(2)}, u32[]{:S(2)}) collective-permute-start(bf16[256,2048]{1,0:T(8,128)(2,1)S(1)} %fusion.25), channel_id=1, source_target_pairs={{0,4},{4,0},{8,12},{12,8},{16,20},{20,16},{24,28},{28,24},{1,5},{5... | collective-permute-start | bytes 3145736 | tf_op jit(solution)/shard_map/ppermute | solution.py:13
  86.8 31.0 %collective-permute-start.22 = (bf16[256,2048]{1,0:T(8,128)(2,1)S(1)}, bf16[256,2048]{1,0:T(8,128)(2,1)S(1)}, u32[]{:S(2)}, u32[]{:S(2)}) collective-permute-start(bf16[256,2048]{1,0:T(8,128)(2,1)S(1)} %fusion.25), channel_id=1, source_target_pairs={{0,8},{4,12},{8,0},{12,4},{16,24},{20,28},{24,16},{28,20},{1,9},{5... | collective-permute-start | bytes 3145736 | tf_op jit(solution)/shard_map/ppermute | solution.py:13
  88.4 3.8 %collective-permute-start.24 = (bf16[256,2048]{1,0:T(8,128)(2,1)S(1)}, bf16[256,2048]{1,0:T(8,128)(2,1)S(1)}, u32[]{:S(2)}, u32[]{:S(2)}) collective-permute-start(bf16[256,2048]{1,0:T(8,128)(2,1)S(1)} %fusion.37), channel_id=1, source_target_pairs={{0,4},{4,0},{8,12},{12,8},{16,20},{20,16},{24,28},{28,24},{1,5},{5... | collective-permute-start | bytes 3145736 | tf_op jit(solution)/shard_map/ppermute | solution.py:13
  89.6 44.2 %collective-permute-start.25 = (bf16[256,2048]{1,0:T(8,128)(2,1)S(1)}, bf16[256,2048]{1,0:T(8,128)(2,1)S(1)}, u32[]{:S(2)}, u32[]{:S(2)}) collective-permute-start(bf16[256,2048]{1,0:T(8,128)(2,1)S(1)} %fusion.37), channel_id=1, source_target_pairs={{0,16},{4,20},{8,24},{12,28},{16,0},{20,4},{24,8},{28,12},{1,17},{... | collective-permute-start | bytes 3145736 | tf_op jit(solution)/shard_map/ppermute | solution.py:13
  97.6 37.6 %collective-permute-start.17 = (bf16[256,2048]{1,0:T(8,128)(2,1)S(1)}, bf16[256,2048]{1,0:T(8,128)(2,1)S(1)}, u32[]{:S(2)}, u32[]{:S(2)}) collective-permute-start(bf16[256,2048]{1,0:T(8,128)(2,1)S(1)} %collective-permute-done.16), channel_id=1, source_target_pairs={{0,4},{4,0},{8,12},{12,8},{16,20},{20,16},{24,28},{28,24},{1,5},{5... | collective-permute-start | bytes 3145736 | tf_op jit(solution)/shard_map/ppermute | solution.py:13
  112.3 24.0 %collective-permute-start.20 = (bf16[256,2048]{1,0:T(8,128)(2,1)S(1)}, bf16[256,2048]{1,0:T(8,128)(2,1)S(1)}, u32[]{:S(2)}, u32[]{:S(2)}) collective-permute-start(bf16[256,2048]{1,0:T(8,128)(2,1)S(1)} %collective-permute-done.19), channel_id=1, source_target_pairs={{0,4},{4,0},{8,12},{12,8},{16,20},{20,16},{24,28},{28,24},{1,5},{5... | collective-permute-start | bytes 3145736 | tf_op jit(solution)/shard_map/ppermute | solution.py:13
  117.8 21.1 %collective-permute-start.23 = (bf16[256,2048]{1,0:T(8,128)(2,1)S(1)}, bf16[256,2048]{1,0:T(8,128)(2,1)S(1)}, u32[]{:S(2)}, u32[]{:S(2)}) collective-permute-start(bf16[256,2048]{1,0:T(8,128)(2,1)S(1)} %collective-permute-done.22), channel_id=1, source_target_pairs={{0,4},{4,0},{8,12},{12,8},{16,20},{20,16},{24,28},{28,24},{1,5},{5... | collective-permute-start | bytes 3145736 | tf_op jit(solution)/shard_map/ppermute | solution.py:13
  133.8 7.7 %collective-permute-start.26 = (bf16[256,2048]{1,0:T(8,128)(2,1)S(1)}, bf16[256,2048]{1,0:T(8,128)(2,1)S(1)}, u32[]{:S(2)}, u32[]{:S(2)}) collective-permute-start(bf16[256,2048]{1,0:T(8,128)(2,1)S(1)} %collective-permute-done.25), channel_id=1, source_target_pairs={{0,4},{4,0},{8,12},{12,8},{16,20},{20,16},{24,28},{28,24},{1,5},{5... | collective-permute-start | bytes 3145736 | tf_op jit(solution)/shard_map/ppermute | solution.py:13
  135.8 14.9 %collective-permute-start.27 = (bf16[128,2048]{1,0:T(8,128)(2,1)S(1)}, bf16[128,2048]{1,0:T(8,128)(2,1)S(1)}, u32[]{:S(2)}, u32[]{:S(2)}) collective-permute-start(bf16[128,2048]{1,0:T(8,128)(2,1)S(1)} %slice.407), channel_id=1, source_target_pairs={{0,16},{4,20},{8,24},{12,28},{16,0},{20,4},{24,8},{28,12},{1,17},{... | collective-permute-start | bytes 1572872 | tf_op jit(solution)/shard_map/ppermute | solution.py:13
  136.8 14.9 %collective-permute-start.28 = (bf16[128,2048]{1,0:T(8,128)(2,1)S(1)}, bf16[128,2048]{1,0:T(8,128)(2,1)S(1)}, u32[]{:S(2)}, u32[]{:S(2)}) collective-permute-start(bf16[128,2048]{1,0:T(8,128)(2,1)S(1)} %slice.406), channel_id=1, source_target_pairs={{0,8},{4,12},{8,0},{12,4},{16,24},{20,28},{24,16},{28,20},{1,9},{5... | collective-permute-start | bytes 1572872 | tf_op jit(solution)/shard_map/ppermute | solution.py:13
  142.4 19.0 %collective-permute-start.29 = (bf16[128,2048]{1,0:T(8,128)(2,1)S(1)}, bf16[128,2048]{1,0:T(8,128)(2,1)S(1)}, u32[]{:S(2)}, u32[]{:S(2)}) collective-permute-start(bf16[128,2048]{1,0:T(8,128)(2,1)S(1)} %slice.405), channel_id=1, source_target_pairs={{0,16},{4,20},{8,24},{12,28},{16,0},{20,4},{24,8},{28,12},{1,17},{... | collective-permute-start | bytes 1572872 | tf_op jit(solution)/shard_map/ppermute | solution.py:13
  143.5 18.8 %collective-permute-start.30 = (bf16[128,2048]{1,0:T(8,128)(2,1)S(1)}, bf16[128,2048]{1,0:T(8,128)(2,1)S(1)}, u32[]{:S(2)}, u32[]{:S(2)}) collective-permute-start(bf16[128,2048]{1,0:T(8,128)(2,1)S(1)} %slice.404), channel_id=1, source_target_pairs={{0,8},{4,12},{8,0},{12,4},{16,24},{20,28},{24,16},{28,20},{1,9},{5... | collective-permute-start | bytes 1572872 | tf_op jit(solution)/shard_map/ppermute | solution.py:13
  (3 other events, 8.2 us)
where the time goes:
time: 165 us
  waiting for transfers between devices  76.4 us (46%)
  starting transfers between devices  35.2 us (21%)
  matrix products  32.1 us (19%)
  other arithmetic  14.2 us (9%)
  local copies, waits for them, and re-layouts  5.5 us (3%)
    ppermute x22, waiting for transfers between devices, xor_send(): return lax.ppermute(value, 'dp', [(i, i ^ mask) for i in range(size)])  60.7 us
    ppermute x6, starting transfers between devices, gather_rows(): lax.ppermute(value, 'tensor', [(i, (i + k) % size) for i in range(size)])  18.3 us
    dot_general x4, matrix products, step_body(): jnp.dot(grad_rows, w_out[:, start:start + step], preferred_element_type=j...  14.4 us
    ppermute x6, waiting for transfers between devices, gather_rows(): lax.ppermute(value, 'tensor', [(i, (i + k) % size) for i in range(size)])  13.3 us
    ppermute x22, starting transfers between devices, xor_send(): return lax.ppermute(value, 'dp', [(i, i ^ mask) for i in range(size)])  11.4 us
    dot_general x1, matrix products, step_body(): lax.dot_general(jnp.concatenate(ordered, axis=1), w_in, (((1,), (1,)), ((...  10.3 us
    dot_general x16, matrix products, transpose_dot(): lax.dot_general(left_rows, right_rows, (((0,), (0,)), ((), ())), preferre...  7.45 us
    ppermute x3, starting transfers between devices, scatter_rows(): lax.ppermute(piece, 'tensor', [(i, (i + k) % size) for i in range(size)])  5.57 us
  transfers between devices with their start and end apart: 31, of which 12 were waited for; matrix products, arithmetic and copies ran while one was open for 21% of the time, Pallas kernels for 0%

commit v1 on v0

--- a/solution.py
+++ b/solution.py
@@ -1,12 +1,16 @@
 import jax
 import jax.numpy as jnp
 from jax import lax
+from jax.experimental import pallas as pl
+from jax.experimental.pallas import tpu as pltpu
 from jax.sharding import PartitionSpec as P
 
 
 momentum_decay = 0.9
 PIECES = 2
 SMALL_AXIS = 8
+TILE = 512
+KERNEL_BYTES = 16 << 20
 
 
 def xor_send(value, size, mask):
@@ -53,10 +57,109 @@
     return masks
 
 
-def transpose_dot(left_rows, right_rows):
-    return lax.dot_general(
-        left_rows, right_rows, (((0,), (0,)), ((), ())), preferred_element_type=jnp.float32
-    )
+def hidden_kernel(grad_ref, saved_ref, w_ref, out_ref):
+    product = jnp.dot(grad_ref[...], w_ref[...], preferred_element_type=jnp.float32)
+    out_ref[...] = jnp.where(saved_ref[...] > 0, product, 0.0).astype(jnp.bfloat16)
+
+
+def hidden_chunk(grad_rows, saved_rows, w_out, start, step):
+    rows, depth = grad_rows.shape
+    tile = min(TILE, step)
+    first = start // tile
+    return pl.pallas_call(
+        hidden_kernel,
+        grid=(step // tile,),
+        out_shape=jax.ShapeDtypeStruct((rows, step), jnp.bfloat16),
+        in_specs=[
+            pl.BlockSpec((rows, depth), lambda j: (0, 0)),
+            pl.BlockSpec((rows, tile), lambda j: (0, first + j)),
+            pl.BlockSpec((depth, tile), lambda j: (0, first + j)),
+        ],
+        out_specs=pl.BlockSpec((rows, tile), lambda j: (0, j)),
+        cost_estimate=pl.CostEstimate(
+            flops=2 * rows * depth * step, bytes_accessed=2 * step * (depth + 2 * rows),
+            transcendentals=0,
+        ),
+        compiler_params=pltpu.CompilerParams(vmem_limit_bytes=KERNEL_BYTES),
+    )(grad_rows, saved_rows, w_out)
+
+
+def gradient_kernel(size, tokens_ref, own_ref, pair_ref, near_ref, far_ref, mom_ref, base_ref, part_ref):
+    width = tokens_ref.shape[0] // 4
+    total = None
+    for i, ref in enumerate((own_ref, pair_ref, near_ref, far_ref)):
+        term = jnp.dot(
+            tokens_ref[i * width:(i + 1) * width, :], ref[...],
+            preferred_element_type=jnp.float32,
+        )
+        total = term if total is None else total + term
+    kept = base_ref.shape[0]
+    base_ref[...] = momentum_decay * mom_ref[...] + total[:kept] / size
+    part_ref[...] = total[kept:].astype(jnp.bfloat16)
+
+
+def gradient_chunk(size, tokens, which, rows_of, mom_in, start):
+    rows, step = rows_of[0].shape
+    kept = mom_in.shape[0]
+    total = tokens.shape[0] // 2
+    width = total // 4
+    tile = min(TILE, step)
+    first = start // tile
+    block = pl.BlockSpec((rows, tile), lambda j: (0, j))
+    return pl.pallas_call(
+        lambda *refs: gradient_kernel(size, *refs),
+        grid=(step // tile,),
+        out_shape=(
+            jax.ShapeDtypeStruct((kept, step), jnp.float32),
+            jax.ShapeDtypeStruct((width - kept, step), jnp.bfloat16),
+        ),
+        in_specs=[
+            pl.BlockSpec((total, rows), lambda j: (which, 0)),
+            block, block, block, block,
+            pl.BlockSpec((kept, tile), lambda j: (0, first + j)),
+        ],
+        out_specs=(
+            pl.BlockSpec((kept, tile), lambda j: (0, j)),
+            pl.BlockSpec((width - kept, tile), lambda j: (0, j)),
+        ),
+        cost_estimate=pl.CostEstimate(
+            flops=2 * rows * total * step, bytes_accessed=8 * rows * step, transcendentals=0
+        ),
+        compiler_params=pltpu.CompilerParams(vmem_limit_bytes=KERNEL_BYTES),
+    )(tokens, *rows_of, mom_in)
+
+
+def finish_kernel(size, count, base_ref, *refs):
+    total = refs[0][...].astype(jnp.float32)
+    for ref in refs[1:count]:
+        total = total + ref[...].astype(jnp.float32)
+    refs[-1][...] = base_ref[...] + total / size
+
+
+def finish_chunk(size, base, parts, start, whole_width, result):
+    kept, step = base.shape
+    tile = min(2 * TILE, step)
+    first = start // tile
+    block = pl.BlockSpec((kept, tile), lambda j: (0, j))
+    operands = [base, *parts]
+    specs = [block] * len(operands)
+    aliases = {}
+    if result is not None:
+        aliases = {len(operands): 0}
+        operands.append(result)
+        specs.append(pl.BlockSpec(memory_space=pl.ANY))
+    return pl.pallas_call(
+        lambda *refs: finish_kernel(size, len(parts), *refs),
+        grid=(step // tile,),
+        out_shape=jax.ShapeDtypeStruct((kept, whole_width), jnp.float32),
+        in_specs=specs,
+        out_specs=pl.BlockSpec((kept, tile), lambda j: (0, first + j)),
+        input_output_aliases=aliases,
+        cost_estimate=pl.CostEstimate(
+            flops=2 * kept * step, bytes_accessed=10 * kept * step, transcendentals=0
+        ),
+        compiler_params=pltpu.CompilerParams(vmem_limit_bytes=KERNEL_BYTES),
+    )(*operands)
 
 
 def step_body(inputs, out_grad, saved, w_in, w_out, mom_in):
@@ -88,8 +191,7 @@
     packed = jnp.concatenate(pieces, axis=2)
     packed, grad_rows = lax.optimization_barrier((packed, grad_rows))
     packed = gather_rows(packed)
-    packed = packed.reshape(-1, packed.shape[2])
-    width = packed.shape[1] // (4 * len(orders))
+    tokens = packed.reshape(-1, packed.shape[2]).T
 
     saved_rows = saved.reshape(-1, hidden_width)
     half = hidden_width // len(orders)
@@ -98,11 +200,7 @@
 
     hidden, near, pair = [], [], []
     for c, (o, start) in enumerate(chunks):
-        product = jnp.dot(
-            grad_rows, w_out[:, start:start + step], preferred_element_type=jnp.float32
-        )
-        mask = saved_rows[:, start:start + step] > 0
-        hidden.append(jnp.where(mask, product, 0.0).astype(jnp.bfloat16))
+        hidden.append(hidden_chunk(grad_rows, saved_rows, w_out, start, step))
         near.append(xor_send(hidden[c], size, orders[o][0]))
         pair.append(xor_send(hidden[c], size, 1))
 
@@ -113,29 +211,22 @@
     ).reshape(micro_count, -1, model_width)
     in_grad = scatter_rows(input_terms)
 
-    new_mom_in = momentum_decay * mom_in
-    arrived = []
+    waiting = []
     for c, (o, start) in enumerate(chunks):
         first, rest = orders[o]
-        tokens = packed[:, o * 4 * width:(o + 1) * 4 * width]
-        terms = [tokens[:, i * width:(i + 1) * width] for i in range(4)]
-        early = transpose_dot(terms[0], hidden[c]) + transpose_dot(terms[1], pair[c])
-        early = lax.optimization_barrier(early)
         near_pair = xor_send(near[c], size, 1)
-        total = early + transpose_dot(terms[2], near[c])
-        total = total + transpose_dot(terms[3], near_pair)
-        kept = total[:own_rows]
-        for i, m in enumerate(spans(rest)):
-            if m:
-                part = total[i * own_rows:(i + 1) * own_rows].astype(jnp.bfloat16)
-                arrived.append((c, xor_send(part, size, m)))
-        old = new_mom_in[:, start:start + step]
-        new_mom_in = new_mom_in.at[:, start:start + step].set(old + kept / size)
-    for c, part in arrived:
-        start = chunks[c][1]
-        old = new_mom_in[:, start:start + step]
-        update = old + part.astype(jnp.float32) / size
-        new_mom_in = new_mom_in.at[:, start:start + step].set(update)
+        base, part = gradient_chunk(
+            size, tokens, o, (hidden[c], pair[c], near[c], near_pair), mom_in, start
+        )
+        parts = [
+            xor_send(part[(i - 1) * own_rows:i * own_rows], size, m)
+            for i, m in enumerate(spans(rest))
+            if m
+        ]
+        waiting.append((start, base, parts))
+    new_mom_in = None
+    for start, base, parts in waiting:
+        new_mom_in = finish_chunk(size, base, parts, start, hidden_width, new_mom_in)
     return (in_grad, new_mom_in)
 
 

time: 165 us -> 1260 us (7.64)
  the two profiles are of different devices: /device:TPU:24 before, /device:TPU:0 now
where the time goes in v1:
time: 1260 us
  local copies, waits for them, and re-layouts  1120 us (89%)
  waiting for transfers between devices  68.8 us (5%)
  Pallas kernels  32 us (3%)
  starting transfers between devices  29.4 us (2%)
    dynamic_update_slice x8, local copies, waits for them, and re-layouts, gather_rows(): full = lax.dynamic_update_slice_in_dim(full, piece, start, axis=1)  1080 us
    ppermute x22, waiting for transfers between devices, xor_send(): return lax.ppermute(value, 'dp', [(i, i ^ mask) for i in range(size)])  46.7 us
    unnamed x57, local copies, waits for them, and re-layouts  30.1 us
  transfers between devices with their start and end apart: 31, of which 9 were waited for; matrix products, arithmetic and copies ran while one was open for 87% of the time, Pallas kernels for 2%

profile of v1, /device:TPU:0, one launch (start us, length us, event | category | flops | bytes accessed | tf_op | source)
XLA Modules:
  0.0 1262.8 jit_solution(10069952458504574779)
XLA Ops:
  0.6 3.1 collective-permute-start.6
  3.7 2.1 collective-permute-start.8
  17.7 2.4 collective-permute-done.4
  20.3 5.8 copy-done
  26.0 2.2 copy-done.3
  28.2 2.3 shard_map.77.refs_1_
  35.1 2.3 shard_map.80.refs_1_
  37.4 2.3 shard_map.79.refs_1_
  39.7 2.3 shard_map.78.refs_1_
  43.6 13.9 %collective-permute-done.13 = bf16[2,32,2048]{2,1,0:T(8,128)(2,1)S(1)} collective-permute-done((bf16[2,32,2048]{2,1,0:T(8,128)(2,1)S(1)}, bf16[2,32,2048]{2,1,0:T(8,128)(2,1)S(1)}, u32[]{:S(2)}, u32[]{:S(2)}) %collective-permute-start.13) | collective-permute-done | bytes 262176 | tf_op jit(solution)/shard_map/ppermute | solution.py:28
  61.7 15.7 %collective-permute-done.20.refs_3_ = bf16[256,2048]{1,0:T(8,128)(2,1)} collective-permute-done((bf16[256,2048]{1,0:T(8,128)(2,1)S(1)}, bf16[256,2048]{1,0:T(8,128)(2,1)}, u32[]{:S(2)}, u32[]{:S(2)}) %collective-permute-start.20) | collective-permute-done | bytes 1048608 | tf_op jit(solution)/shard_map/ppermute | solution.py:17
  78.9 4.8 collective-permute-done.24.refs_3_
  83.8 21.9 %collective-permute-done.16.refs_3_ = bf16[256,2048]{1,0:T(8,128)(2,1)} collective-permute-done((bf16[256,2048]{1,0:T(8,128)(2,1)S(1)}, bf16[256,2048]{1,0:T(8,128)(2,1)}, u32[]{:S(2)}, u32[]{:S(2)}) %collective-permute-start.16) | collective-permute-done | bytes 1048608 | tf_op jit(solution)/shard_map/ppermute | solution.py:17
  107.2 11.3 fusion
  119.5 2.0 copy.11
  122.8 62.3 %dynamic_update_slice.28 = bf16[2,128,2048]{1,0,2:T(2,128)(2,1)} dynamic-update-slice(bf16[2,128,2048]{1,0,2:T(2,128)(2,1)} %broadcast_in_dim.7, bf16[2,32,2048]{1,0,2:T(2,128)(2,1)} %copy.11, s32[]{:T(128)} %constant.64.clone.1, s32[]{:T(128)S(6)} %select_n.108, s32[]{:T(128)} %constant.64.clone.1) | dynamic-update-slice | bytes 524292 | tf_op jit(solution)/shard_map/dynamic_update_slice | solution.py:34
  187.0 2.0 copy.12
  189.0 337.7 %dynamic_update_slice.29 = bf16[2,128,2048]{1,0,2:T(2,128)(2,1)} dynamic-update-slice(bf16[2,128,2048]{1,0,2:T(2,128)(2,1)} %dynamic_update_slice.28, bf16[2,32,2048]{1,0,2:T(2,128)(2,1)} %copy.12, s32[]{:T(128)} %constant.64.clone.1, s32[]{:T(128)S(6)} %select_n.110, s32[]{:T(128)} %constant.64.clone.1) | dynamic-update-slice | bytes 524292 | tf_op jit(solution)/shard_map/dynamic_update_slice | solution.py:34
  526.7 2.0 copy.13
  528.7 337.7 %dynamic_update_slice.30 = bf16[2,128,2048]{1,0,2:T(2,128)(2,1)} dynamic-update-slice(bf16[2,128,2048]{1,0,2:T(2,128)(2,1)} %dynamic_update_slice.29, bf16[2,32,2048]{1,0,2:T(2,128)(2,1)} %copy.13, s32[]{:T(128)} %constant.64.clone.1, s32[]{:T(128)S(6)} %select_n.112, s32[]{:T(128)} %constant.64.clone.1) | dynamic-update-slice | bytes 524292 | tf_op jit(solution)/shard_map/dynamic_update_slice | solution.py:34
  866.4 2.0 copy.14
  868.4 337.7 %dynamic_update_slice.31 = bf16[2,128,2048]{1,0,2:T(2,128)(2,1)} dynamic-update-slice(bf16[2,128,2048]{1,0,2:T(2,128)(2,1)} %dynamic_update_slice.30, bf16[2,32,2048]{1,0,2:T(2,128)(2,1)} %copy.14, s32[]{:T(128)} %constant.64.clone.1, s32[]{:T(128)S(6)} %select_n.114, s32[]{:T(128)} %constant.64.clone.1) | dynamic-update-slice | bytes 524292 | tf_op jit(solution)/shard_map/dynamic_update_slice | solution.py:34
  1207.5 2.2 copy-done.1
  1214.6 3.0 shard_map.84
  1221.4 4.4 shard_map.82
  1228.8 4.5 shard_map.83
  1235.1 4.5 shard_map.81
  1240.0 3.5 collective-permute-start.11
  1243.4 2.8 collective-permute-done.11
  1247.0 5.4 collective-permute-done.10
  1255.3 2.0 shard_map.85.refs_2_
  1258.5 2.0 shard_map.86.refs_2_
  (123 shorter events, 51.6 us)
Async XLA Ops:
  0.6 19.5 %collective-permute-start.6 = (bf16[2,32,1024]{2,1,0:T(8,128)(2,1)}, bf16[2,32,1024]{2,1,0:T(8,128)(2,1)S(1)}, u32[]{:S(2)}, u32[]{:S(2)}) collective-permute-start(bf16[2,32,1024]{2,1,0:T(8,128)(2,1)} %param.7), channel_id=1, source_target_pairs={{0,1},{1,2},{2,3},{3,0},{4,5},{5,6},{6,7},{7,4},{8,9},{9,10},{10,1... | collective-permute-start | bytes 393224 | tf_op jit(solution)/shard_map/ppermute | solution.py:28
  3.7 16.5 %collective-permute-start.8 = (bf16[2,32,1024]{2,1,0:T(8,128)(2,1)}, bf16[2,32,1024]{2,1,0:T(8,128)(2,1)S(1)}, u32[]{:S(2)}, u32[]{:S(2)}) collective-permute-start(bf16[2,32,1024]{2,1,0:T(8,128)(2,1)} %param.7), channel_id=1, source_target_pairs={{0,3},{1,0},{2,1},{3,2},{4,7},{5,4},{6,5},{7,6},{8,11},{9,8},{10,9... | collective-permute-start | bytes 393224 | tf_op jit(solution)/shard_map/ppermute | solution.py:28
  5.8 14.4 %collective-permute-start.7 = (bf16[2,32,1024]{2,1,0:T(8,128)(2,1)}, bf16[2,32,1024]{2,1,0:T(8,128)(2,1)S(1)}, u32[]{:S(2)}, u32[]{:S(2)}) collective-permute-start(bf16[2,32,1024]{2,1,0:T(8,128)(2,1)} %param.7), channel_id=1, source_target_pairs={{0,2},{1,3},{2,0},{3,1},{4,6},{5,7},{6,4},{7,5},{8,10},{9,11},{10,... | collective-permute-start | bytes 393224 | tf_op jit(solution)/shard_map/ppermute | solution.py:28
  7.7 4.2 collective-permute-start.1
  9.3 1.9 collective-permute-start
  11.2 3.4 collective-permute-start.2
  11.8 8.3 collective-permute-start.5
  14.6 1.6 collective-permute-start.3
  16.2 3.9 collective-permute-start.4
  30.5 28.6 %collective-permute-start.28 = (bf16[256,2048]{1,0:T(8,128)(2,1)S(1)}, bf16[256,2048]{1,0:T(8,128)(2,1)S(1)}, u32[]{:S(2)}, u32[]{:S(2)}) collective-permute-start(bf16[256,2048]{1,0:T(8,128)(2,1)S(1)} %shard_map.77.refs_1_), channel_id=1, source_target_pairs={{0,8},{4,12},{8,0},{12,4},{16,24},{20,28},{24,16},{28,20},{1,9},{5... | collective-permute-start | bytes 3145736 | tf_op jit(solution)/shard_map/ppermute | solution.py:17
  30.8 28.9 %collective-permute-start.27 = (bf16[256,2048]{1,0:T(8,128)(2,1)S(1)}, bf16[256,2048]{1,0:T(8,128)(2,1)S(1)}, u32[]{:S(2)}, u32[]{:S(2)}) collective-permute-start(bf16[256,2048]{1,0:T(8,128)(2,1)S(1)} %shard_map.77.refs_1_), channel_id=1, source_target_pairs={{0,4},{4,0},{8,12},{12,8},{16,20},{20,16},{24,28},{28,24},{1,5},{5... | collective-permute-start | bytes 3145736 | tf_op jit(solution)/shard_map/ppermute | solution.py:17
  30.8 11.2 collective-permute-start.14
  32.1 25.4 %collective-permute-start.13 = (bf16[2,32,2048]{2,1,0:T(8,128)(2,1)S(1)}, bf16[2,32,2048]{2,1,0:T(8,128)(2,1)S(1)}, u32[]{:S(2)}, u32[]{:S(2)}) collective-permute-start(bf16[2,32,2048]{2,1,0:T(8,128)(2,1)S(1)} %constant_dynamic-update-slice_fusion), channel_id=1, source_target_pairs={{0,2},{1,3},{2,0},{3,1},{4,6},{5,7},{6,4},{7,5},{8,10},{9,11},{10,... | collective-permute-start | bytes 786440 | tf_op jit(solution)/shard_map/ppermute | solution.py:28
  34.0 23.6 %collective-permute-start.12 = (bf16[2,32,2048]{2,1,0:T(8,128)(2,1)S(1)}, bf16[2,32,2048]{2,1,0:T(8,128)(2,1)S(1)}, u32[]{:S(2)}, u32[]{:S(2)}) collective-permute-start(bf16[2,32,2048]{2,1,0:T(8,128)(2,1)S(1)} %constant_dynamic-update-slice_fusion), channel_id=1, source_target_pairs={{0,1},{1,2},{2,3},{3,0},{4,5},{5,6},{6,7},{7,4},{8,9},{9,10},{10,1... | collective-permute-start | bytes 786440 | tf_op jit(solution)/shard_map/ppermute | solution.py:28
  42.1 35.4 %collective-permute-start.20 = (bf16[256,2048]{1,0:T(8,128)(2,1)S(1)}, bf16[256,2048]{1,0:T(8,128)(2,1)}, u32[]{:S(2)}, u32[]{:S(2)}) collective-permute-start(bf16[256,2048]{1,0:T(8,128)(2,1)S(1)} %shard_map.78.refs_1_), channel_id=1, source_target_pairs={{0,8},{4,12},{8,0},{12,4},{16,24},{20,28},{24,16},{28,20},{1,9},{5... | collective-permute-start | bytes 3145736 | tf_op jit(solution)/shard_map/ppermute | solution.py:17
  57.5 19.9 %collective-permute-start.19 = (bf16[256,2048]{1,0:T(8,128)(2,1)S(1)}, bf16[256,2048]{1,0:T(8,128)(2,1)S(1)}, u32[]{:S(2)}, u32[]{:S(2)}) collective-permute-start(bf16[256,2048]{1,0:T(8,128)(2,1)S(1)} %shard_map.78.refs_1_), channel_id=1, source_target_pairs={{0,4},{4,0},{8,12},{12,8},{16,20},{20,16},{24,28},{28,24},{1,5},{5... | collective-permute-start | bytes 3145736 | tf_op jit(solution)/shard_map/ppermute | solution.py:17
  57.5 26.2 %collective-permute-start.24 = (bf16[256,2048]{1,0:T(8,128)(2,1)S(1)}, bf16[256,2048]{1,0:T(8,128)(2,1)}, u32[]{:S(2)}, u32[]{:S(2)}) collective-permute-start(bf16[256,2048]{1,0:T(8,128)(2,1)S(1)} %shard_map.79.refs_1_), channel_id=1, source_target_pairs={{0,16},{4,20},{8,24},{12,28},{16,0},{20,4},{24,8},{28,12},{1,17},{... | collective-permute-start | bytes 3145736 | tf_op jit(solution)/shard_map/ppermute | solution.py:17
  59.1 46.6 %collective-permute-start.16 = (bf16[256,2048]{1,0:T(8,128)(2,1)S(1)}, bf16[256,2048]{1,0:T(8,128)(2,1)}, u32[]{:S(2)}, u32[]{:S(2)}) collective-permute-start(bf16[256,2048]{1,0:T(8,128)(2,1)S(1)} %shard_map.80.refs_1_), channel_id=1, source_target_pairs={{0,16},{4,20},{8,24},{12,28},{16,0},{20,4},{24,8},{28,12},{1,17},{... | collective-permute-start | bytes 3145736 | tf_op jit(solution)/shard_map/ppermute | solution.py:17
  60.6 45.1 %collective-permute-start.29 = (bf16[256,2048]{1,0:T(8,128)(2,1)S(1)}, bf16[256,2048]{1,0:T(8,128)(2,1)S(1)}, u32[]{:S(2)}, u32[]{:S(2)}) collective-permute-start(bf16[256,2048]{1,0:T(8,128)(2,1)S(1)} %collective-permute-done.28.refs_3_), channel_id=1, source_target_pairs={{0,4},{4,0},{8,12},{12,8},{16,20},{20,16},{24,28},{28,24},{1,5},{5... | collective-permute-start | bytes 3145736 | tf_op jit(solution)/shard_map/ppermute | solution.py:17
  77.4 1149.3 %collective-permute-start.23 = (bf16[256,2048]{1,0:T(8,128)(2,1)S(1)}, bf16[256,2048]{1,0:T(8,128)(2,1)}, u32[]{:S(2)}, u32[]{:S(2)}) collective-permute-start(bf16[256,2048]{1,0:T(8,128)(2,1)S(1)} %shard_map.79.refs_1_), channel_id=1, source_target_pairs={{0,4},{4,0},{8,12},{12,8},{16,20},{20,16},{24,28},{28,24},{1,5},{5... | collective-permute-start | bytes 3145736 | tf_op jit(solution)/shard_map/ppermute | solution.py:17
  78.4 1154.9 %collective-permute-start.15 = (bf16[256,2048]{1,0:T(8,128)(2,1)S(1)}, bf16[256,2048]{1,0:T(8,128)(2,1)}, u32[]{:S(2)}, u32[]{:S(2)}) collective-permute-start(bf16[256,2048]{1,0:T(8,128)(2,1)S(1)} %shard_map.80.refs_1_), channel_id=1, source_target_pairs={{0,4},{4,0},{8,12},{12,8},{16,20},{20,16},{24,28},{28,24},{1,5},{5... | collective-permute-start | bytes 3145736 | tf_op jit(solution)/shard_map/ppermute | solution.py:17
  83.8 1134.8 %collective-permute-start.21 = (bf16[256,2048]{1,0:T(8,128)(2,1)}, bf16[256,2048]{1,0:T(8,128)(2,1)}, u32[]{:S(2)}, u32[]{:S(2)}) collective-permute-start(bf16[256,2048]{1,0:T(8,128)(2,1)} %collective-permute-done.20.refs_3_), channel_id=1, source_target_pairs={{0,4},{4,0},{8,12},{12,8},{16,20},{20,16},{24,28},{28,24},{1,5},{5... | collective-permute-start | bytes 3145736 | tf_op jit(solution)/shard_map/ppermute | solution.py:17
  105.7 1122.6 %collective-permute-start.25 = (bf16[256,2048]{1,0:T(8,128)(2,1)}, bf16[256,2048]{1,0:T(8,128)(2,1)}, u32[]{:S(2)}, u32[]{:S(2)}) collective-permute-start(bf16[256,2048]{1,0:T(8,128)(2,1)} %collective-permute-done.24.refs_3_), channel_id=1, source_target_pairs={{0,4},{4,0},{8,12},{12,8},{16,20},{20,16},{24,28},{28,24},{1,5},{5... | collective-permute-start | bytes 3145736 | tf_op jit(solution)/shard_map/ppermute | solution.py:17
  106.7 1128.4 %collective-permute-start.17 = (bf16[256,2048]{1,0:T(8,128)(2,1)}, bf16[256,2048]{1,0:T(8,128)(2,1)}, u32[]{:S(2)}, u32[]{:S(2)}) collective-permute-start(bf16[256,2048]{1,0:T(8,128)(2,1)} %collective-permute-done.16.refs_3_), channel_id=1, source_target_pairs={{0,4},{4,0},{8,12},{12,8},{16,20},{20,16},{24,28},{28,24},{1,5},{5... | collective-permute-start | bytes 3145736 | tf_op jit(solution)/shard_map/ppermute | solution.py:17
  107.2 79.8 %copy-start.23 = (bf16[2,32,2048]{2,1,0:T(8,128)(2,1)S(1)}, bf16[2,32,2048]{2,1,0:T(8,128)(2,1)}, u32[]{:S(2)}) copy-start(bf16[2,32,2048]{2,1,0:T(8,128)(2,1)} %copy-done.22) | copy-start | bytes 786436
  1218.6 21.4 %collective-permute-start.9 = (bf16[2,32,1024]{2,1,0:T(8,128)(2,1)}, bf16[2,32,1024]{2,1,0:T(8,128)(2,1)S(1)}, u32[]{:S(2)}, u32[]{:S(2)}) collective-permute-start(bf16[2,32,1024]{2,1,0:T(8,128)(2,1)} %get-tuple-element.24), channel_id=1, source_target_pairs={{0,1},{1,2},{2,3},{3,0},{4,5},{5,6},{6,7},{7,4},{8,9},{9,10},{10,1... | collective-permute-start | bytes 393224 | tf_op jit(solution)/shard_map/ppermute | solution.py:48
  1226.8 27.3 %collective-permute-start.30 = (bf16[128,2048]{1,0:T(8,128)(2,1)}, bf16[128,2048]{1,0:T(8,128)(2,1)}, u32[]{:S(2)}, u32[]{:S(2)}) collective-permute-start(bf16[128,2048]{1,0:T(8,128)(2,1)} %get-tuple-element.21), channel_id=1, source_target_pairs={{0,16},{4,20},{8,24},{12,28},{16,0},{20,4},{24,8},{28,12},{1,17},{... | collective-permute-start | bytes 1572872 | tf_op jit(solution)/shard_map/ppermute | solution.py:17
  1228.3 32.3 %collective-permute-start.22 = (bf16[128,2048]{1,0:T(8,128)(2,1)}, bf16[128,2048]{1,0:T(8,128)(2,1)S(1)}, u32[]{:S(2)}, u32[]{:S(2)}) collective-permute-start(bf16[128,2048]{1,0:T(8,128)(2,1)} %get-tuple-element.17), channel_id=1, source_target_pairs={{0,16},{4,20},{8,24},{12,28},{16,0},{20,4},{24,8},{28,12},{1,17},{... | collective-permute-start | bytes 1572872 | tf_op jit(solution)/shard_map/ppermute | solution.py:17
  1233.3 24.0 %collective-permute-start.26 = (bf16[128,2048]{1,0:T(8,128)(2,1)}, bf16[128,2048]{1,0:T(8,128)(2,1)}, u32[]{:S(2)}, u32[]{:S(2)}) collective-permute-start(bf16[128,2048]{1,0:T(8,128)(2,1)} %get-tuple-element.19), channel_id=1, source_target_pairs={{0,8},{4,12},{8,0},{12,4},{16,24},{20,28},{24,16},{28,20},{1,9},{5... | collective-permute-start | bytes 1572872 | tf_op jit(solution)/shard_map/ppermute | solution.py:17
  1239.6 22.1 %collective-permute-start.18 = (bf16[128,2048]{1,0:T(8,128)(2,1)}, bf16[128,2048]{1,0:T(8,128)(2,1)S(1)}, u32[]{:S(2)}, u32[]{:S(2)}) collective-permute-start(bf16[128,2048]{1,0:T(8,128)(2,1)} %get-tuple-element.15), channel_id=1, source_target_pairs={{0,8},{4,12},{8,0},{12,4},{16,24},{20,28},{24,16},{28,20},{1,9},{5... | collective-permute-start | bytes 1572872 | tf_op jit(solution)/shard_map/ppermute | solution.py:17
  1240.0 6.3 collective-permute-start.11
  1246.3 6.1 collective-permute-start.10
  (23 other events, 195.8 us)

commit v2 on v1

--- a/solution.py
+++ b/solution.py
@@ -2,7 +2,6 @@
 import jax.numpy as jnp
 from jax import lax
 from jax.experimental import pallas as pl
-from jax.experimental.pallas import tpu as pltpu
 from jax.sharding import PartitionSpec as P
 
 
@@ -10,7 +9,6 @@
 PIECES = 2
 SMALL_AXIS = 8
 TILE = 512
-KERNEL_BYTES = 16 << 20
 
 
 def xor_send(value, size, mask):
@@ -80,16 +78,15 @@
             flops=2 * rows * depth * step, bytes_accessed=2 * step * (depth + 2 * rows),
             transcendentals=0,
         ),
-        compiler_params=pltpu.CompilerParams(vmem_limit_bytes=KERNEL_BYTES),
     )(grad_rows, saved_rows, w_out)
 
 
 def gradient_kernel(size, tokens_ref, own_ref, pair_ref, near_ref, far_ref, mom_ref, base_ref, part_ref):
-    width = tokens_ref.shape[0] // 4
+    width = tokens_ref.shape[1] // 4
     total = None
     for i, ref in enumerate((own_ref, pair_ref, near_ref, far_ref)):
-        term = jnp.dot(
-            tokens_ref[i * width:(i + 1) * width, :], ref[...],
+        term = lax.dot_general(
+            tokens_ref[:, i * width:(i + 1) * width], ref[...], (((0,), (0,)), ((), ())),
             preferred_element_type=jnp.float32,
         )
         total = term if total is None else total + term
@@ -101,7 +98,7 @@
 def gradient_chunk(size, tokens, which, rows_of, mom_in, start):
     rows, step = rows_of[0].shape
     kept = mom_in.shape[0]
-    total = tokens.shape[0] // 2
+    total = tokens.shape[1] // 2
     width = total // 4
     tile = min(TILE, step)
     first = start // tile
@@ -114,7 +111,7 @@
             jax.ShapeDtypeStruct((width - kept, step), jnp.bfloat16),
         ),
         in_specs=[
-            pl.BlockSpec((total, rows), lambda j: (which, 0)),
+            pl.BlockSpec((rows, total), lambda j: (0, which)),
             block, block, block, block,
             pl.BlockSpec((kept, tile), lambda j: (0, first + j)),
         ],
@@ -125,7 +122,6 @@
         cost_estimate=pl.CostEstimate(
             flops=2 * rows * total * step, bytes_accessed=8 * rows * step, transcendentals=0
         ),
-        compiler_params=pltpu.CompilerParams(vmem_limit_bytes=KERNEL_BYTES),
     )(tokens, *rows_of, mom_in)
 
 
@@ -158,7 +154,6 @@
         cost_estimate=pl.CostEstimate(
             flops=2 * kept * step, bytes_accessed=10 * kept * step, transcendentals=0
         ),
-        compiler_params=pltpu.CompilerParams(vmem_limit_bytes=KERNEL_BYTES),
     )(*operands)
 
 
@@ -191,7 +186,7 @@
     packed = jnp.concatenate(pieces, axis=2)
     packed, grad_rows = lax.optimization_barrier((packed, grad_rows))
     packed = gather_rows(packed)
-    tokens = packed.reshape(-1, packed.shape[2]).T
+    tokens = packed.reshape(-1, packed.shape[2])
 
     saved_rows = saved.reshape(-1, hidden_width)
     half = hidden_width // len(orders)

time: 1260 us -> 160 us (0.13)
  local copies, waits for them, and re-layouts: 1120 us -> 11.5 us
  Pallas kernels: 32 us -> 51.7 us
  waiting for transfers between devices: 68.8 us -> 52.7 us
    dynamic_update_slice x8, local copies, waits for them, and re-layouts: 1080 us -> 3.92 us  [gather_rows(): full = lax.dynamic_update_slice_in_dim(full, piece, start, axis=1)]
    unnamed x57 -> x34, local copies, waits for them, and re-layouts: 30.1 us -> 6.48 us
  transfers between devices with their start and end apart: 31 -> 31, of which waited for: 9 -> 9; matrix products, arithmetic and copies ran while one was open for 87% -> 12% of each run, Pallas kernels for 2% -> 28%
where the time goes in v2:
time: 160 us; the launch traced here: 159 us
  waiting for transfers between devices  52.7 us (33%)
  Pallas kernels  51.7 us (32%)
  starting transfers between devices  29.5 us (18%)
  local copies, waits for them, and re-layouts  11.5 us (7%)
  matrix products  10.6 us (7%)
  other arithmetic  1.75 us (1%)
    ppermute x22, waiting for transfers between devices, xor_send(): return lax.ppermute(value, 'dp', [(i, i ^ mask) for i in range(size)])  38.9 us
    pallas_call x4, Pallas kernels, gradient_chunk(): pl.pallas_call(lambda *refs: gradient_kernel(size, *refs), grid=(step //...  22 us
    pallas_call x4, Pallas kernels, hidden_chunk(): pl.pallas_call(hidden_kernel, grid=(step // tile,), out_shape=jax.ShapeDt...  20.9 us
    ppermute x22, starting transfers between devices, xor_send(): return lax.ppermute(value, 'dp', [(i, i ^ mask) for i in range(size)])  14.7 us
    dot_general x1, matrix products, step_body(): lax.dot_general(jnp.concatenate(ordered, axis=1), w_in, (((1,), (1,)), ((...  10.6 us
    ppermute x6, starting transfers between devices, gather_rows(): lax.ppermute(value, 'tensor', [(i, (i + k) % size) for i in range(size)])  10.4 us
    pallas_call x4, Pallas kernels, finish_chunk(): pl.pallas_call(lambda *refs: finish_kernel(size, len(parts), *refs), grid...  8.77 us
    ppermute x3, waiting for transfers between devices, scatter_rows(): lax.ppermute(piece, 'tensor', [(i, (i + k) % size) for i in range(size)])  8.46 us
  transfers between devices with their start and end apart: 31, of which 9 were waited for; matrix products, arithmetic and copies ran while one was open for 12% of the time, Pallas kernels for 28%

profile of v2, /device:TPU:0, one launch (start us, length us, event | category | flops | bytes accessed | tf_op | source)
XLA Modules:
  0.0 158.7 jit_solution(4774526649714888117)
XLA Ops:
  0.6 3.1 %collective-permute-start.6 = (bf16[2,32,1024]{2,1,0:T(8,128)(2,1)}, bf16[2,32,1024]{2,1,0:T(8,128)(2,1)S(1)}, u32[]{:S(2)}, u32[]{:S(2)}) collective-permute-start(bf16[2,32,1024]{2,1,0:T(8,128)(2,1)} %param.7), channel_id=1, source_target_pairs={{0,1},{1,2},{2,3},{3,0},{4,5},{5,6},{6,7},{7,4},{8,9},{9,10},{10,1... | collective-permute-start | bytes 393224 | tf_op jit(solution)/shard_map/ppermute | solution.py:26
  3.7 2.1 %collective-permute-start.8 = (bf16[2,32,1024]{2,1,0:T(8,128)(2,1)}, bf16[2,32,1024]{2,1,0:T(8,128)(2,1)S(1)}, u32[]{:S(2)}, u32[]{:S(2)}) collective-permute-start(bf16[2,32,1024]{2,1,0:T(8,128)(2,1)} %param.7), channel_id=1, source_target_pairs={{0,3},{1,0},{2,1},{3,2},{4,7},{5,4},{6,5},{7,6},{8,11},{9,8},{10,9... | collective-permute-start | bytes 393224 | tf_op jit(solution)/shard_map/ppermute | solution.py:26
  7.7 1.6 collective-permute-start.1
  13.0 1.6 collective-permute-done.2
  16.2 1.5 collective-permute-start.4
  17.7 2.4 %collective-permute-done.4 = bf16[2,32,256]{2,1,0:T(8,128)(2,1)S(1)} collective-permute-done((bf16[2,32,256]{2,1,0:T(8,128)(2,1)S(1)}, bf16[2,32,256]{2,1,0:T(8,128)(2,1)S(1)}, u32[]{:S(2)}, u32[]{:S(2)}) %collective-permute-start.4) | collective-permute-done | bytes 32800 | tf_op jit(solution)/shard_map/ppermute | solution.py:15
  21.1 5.2 %shard_map.77.refs_1_ = bf16[256,2048]{1,0:T(8,128)(2,1)} custom-call(bf16[256,1024]{1,0:T(8,128)(2,1)} %bitcast.13, bf16[256,8192]{1,0:T(8,128)(2,1)} %bitcast.5, bf16[1024,8192]{1,0:T(8,128)(2,1)} %w_ref.7), custom_call_target="tpu_custom_call" | custom-call | flops 1073741824 | bytes 6291456 | tf_op jit(solution)/shard_map/pallas_call | solution.py:67
  27.8 1.8 %collective-permute-start.13 = (bf16[2,32,2048]{2,1,0:T(8,128)(2,1)S(1)}, bf16[2,32,2048]{2,1,0:T(8,128)(2,1)}, u32[]{:S(2)}, u32[]{:S(2)}) collective-permute-start(bf16[2,32,2048]{2,1,0:T(8,128)(2,1)S(1)} %constant_dynamic-update-slice_fusion), channel_id=1, source_target_pairs={{0,2},{1,3},{2,0},{3,1},{4,6},{5,7},{6,4},{7,5},{8,10},{9,11},{10,... | collective-permute-start | bytes 786440 | tf_op jit(solution)/shard_map/ppermute | solution.py:26
  30.8 5.1 %shard_map.80.refs_1_ = bf16[256,2048]{1,0:T(8,128)(2,1)} custom-call(bf16[256,1024]{1,0:T(8,128)(2,1)} %bitcast.14, bf16[256,8192]{1,0:T(8,128)(2,1)} %bitcast.6, bf16[1024,8192]{1,0:T(8,128)(2,1)} %w_ref.7), custom_call_target="tpu_custom_call" | custom-call | flops 1073741824 | bytes 6291456 | tf_op jit(solution)/shard_map/pallas_call | solution.py:67
  35.9 5.2 %shard_map.79.refs_1_ = bf16[256,2048]{1,0:T(8,128)(2,1)} custom-call(bf16[256,1024]{1,0:T(8,128)(2,1)} %bitcast.15, bf16[256,8192]{1,0:T(8,128)(2,1)} %bitcast.7, bf16[1024,8192]{1,0:T(8,128)(2,1)} %w_ref.7), custom_call_target="tpu_custom_call" | custom-call | flops 1073741824 | bytes 6291456 | tf_op jit(solution)/shard_map/pallas_call | solution.py:67
  41.2 5.3 %shard_map.78.refs_1_ = bf16[256,2048]{1,0:T(8,128)(2,1)} custom-call(bf16[256,1024]{1,0:T(8,128)(2,1)} %bitcast.16, bf16[256,8192]{1,0:T(8,128)(2,1)} %bitcast.8, bf16[1024,8192]{1,0:T(8,128)(2,1)} %w_ref.7), custom_call_target="tpu_custom_call" | custom-call | flops 1073741824 | bytes 6291456 | tf_op jit(solution)/shard_map/pallas_call | solution.py:67
  46.5 1.5 collective-permute-start.20
  48.0 5.3 %collective-permute-done.13 = bf16[2,32,2048]{2,1,0:T(8,128)(2,1)} collective-permute-done((bf16[2,32,2048]{2,1,0:T(8,128)(2,1)S(1)}, bf16[2,32,2048]{2,1,0:T(8,128)(2,1)}, u32[]{:S(2)}, u32[]{:S(2)}) %collective-permute-start.13) | collective-permute-done | bytes 262176 | tf_op jit(solution)/shard_map/ppermute | solution.py:26
  53.3 1.6 collective-permute-start.24
  55.5 10.6 %fusion = f32[256,1024]{1,0:T(8,128)S(1)} fusion(bf16[1024,8192]{1,0:T(8,128)(2,1)} %param.9, bf16[256,2048]{1,0:T(8,128)(2,1)S(1)} %copy-done.2, bf16[256,2048]{1,0:T(8,128)(2,1)S(1)} %copy-done.3, bf16[256,2048]{1,0:T(8,128)(2,1)} %shard_map.78.refs_1_, bf16[256,2048]{1,0:T(8,128)(2,1)S(1)} %copy-done.4), kind=kOutput, calls=%fused_computation | convolution fusion | flops 4311744512 | bytes 22020096 | tf_op jit(solution)/shard_map/dot_general | solution.py:203
  66.1 7.2 %collective-permute-done.20.refs_3_ = bf16[256,2048]{1,0:T(8,128)(2,1)} collective-permute-done((bf16[256,2048]{1,0:T(8,128)(2,1)}, bf16[256,2048]{1,0:T(8,128)(2,1)}, u32[]{:S(2)}, u32[]{:S(2)}) %collective-permute-start.20) | collective-permute-done | bytes 1048608 | tf_op jit(solution)/shard_map/ppermute | solution.py:15
  73.8 5.7 %collective-permute-done.24.refs_3_ = bf16[256,2048]{1,0:T(8,128)(2,1)} collective-permute-done((bf16[256,2048]{1,0:T(8,128)(2,1)S(1)}, bf16[256,2048]{1,0:T(8,128)(2,1)}, u32[]{:S(2)}, u32[]{:S(2)}) %collective-permute-start.24) | collective-permute-done | bytes 1048608 | tf_op jit(solution)/shard_map/ppermute | solution.py:15
  79.7 21.8 %collective-permute-done.16.refs_3_ = bf16[256,2048]{1,0:T(8,128)(2,1)} collective-permute-done((bf16[256,2048]{1,0:T(8,128)(2,1)S(1)}, bf16[256,2048]{1,0:T(8,128)(2,1)}, u32[]{:S(2)}, u32[]{:S(2)}) %collective-permute-start.16) | collective-permute-done | bytes 1048608 | tf_op jit(solution)/shard_map/ppermute | solution.py:15
  106.0 5.5 %shard_map.84 = (f32[128,2048]{1,0:T(8,128)}, bf16[128,2048]{1,0:T(8,128)(2,1)}) custom-call(bf16[256,2048]{1,0:T(8,128)(2,1)} %bitcast.9, bf16[256,2048]{1,0:T(8,128)(2,1)} %shard_map.77.refs_1_, bf16[256,2048]{1,0:T(8,128)(2,1)} %collective-permute-done.27.refs_2_, bf16[256,2048]{1,0:T(8,128)(2,1)} %collective-permute-done.28.refs_3_, ...), custom_call_target="tpu_custom_call" | custom-call | flops 1073741824 | bytes 4194304 | tf_op jit(solution)/shard_map/pallas_call | solution.py:106
  111.6 5.6 %shard_map.82 = (f32[128,2048]{1,0:T(8,128)}, bf16[128,2048]{1,0:T(8,128)(2,1)}) custom-call(bf16[256,2048]{1,0:T(8,128)(2,1)} %bitcast.10, bf16[256,2048]{1,0:T(8,128)(2,1)} %shard_map.78.refs_1_, bf16[256,2048]{1,0:T(8,128)(2,1)} %copy-done.5, bf16[256,2048]{1,0:T(8,128)(2,1)} %collective-permute-done.20.refs_3_, ...), custom_call_target="tpu_custom_call" | custom-call | flops 1073741824 | bytes 4194304 | tf_op jit(solution)/shard_map/pallas_call | solution.py:106
  117.2 1.6 %collective-permute-start.30 = (bf16[128,2048]{1,0:T(8,128)(2,1)S(1)}, bf16[128,2048]{1,0:T(8,128)(2,1)S(1)}, u32[]{:S(2)}, u32[]{:S(2)}) collective-permute-start(bf16[128,2048]{1,0:T(8,128)(2,1)S(1)} %copy-done.12), channel_id=1, source_target_pairs={{0,16},{4,20},{8,24},{12,28},{16,0},{20,4},{24,8},{28,12},{1,17},{... | collective-permute-start | bytes 1572872 | tf_op jit(solution)/shard_map/ppermute | solution.py:15
  119.3 5.4 %shard_map.83 = (f32[128,2048]{1,0:T(8,128)}, bf16[128,2048]{1,0:T(8,128)(2,1)}) custom-call(bf16[256,2048]{1,0:T(8,128)(2,1)} %bitcast.11, bf16[256,2048]{1,0:T(8,128)(2,1)} %shard_map.79.refs_1_, bf16[256,2048]{1,0:T(8,128)(2,1)} %collective-permute-done.23.refs_2_, bf16[256,2048]{1,0:T(8,128)(2,1)} %collective-permute-done.24.refs_3_, ...), custom_call_target="tpu_custom_call" | custom-call | flops 1073741824 | bytes 4194304 | tf_op jit(solution)/shard_map/pallas_call | solution.py:106
  124.7 1.7 %collective-permute-start.26 = (bf16[128,2048]{1,0:T(8,128)(2,1)}, bf16[128,2048]{1,0:T(8,128)(2,1)S(1)}, u32[]{:S(2)}, u32[]{:S(2)}) collective-permute-start(bf16[128,2048]{1,0:T(8,128)(2,1)} %get-tuple-element.19), channel_id=1, source_target_pairs={{0,8},{4,12},{8,0},{12,4},{16,24},{20,28},{24,16},{28,20},{1,9},{5... | collective-permute-start | bytes 1572872 | tf_op jit(solution)/shard_map/ppermute | solution.py:15
  126.5 5.4 %shard_map.81 = (f32[128,2048]{1,0:T(8,128)}, bf16[128,2048]{1,0:T(8,128)(2,1)}) custom-call(bf16[256,2048]{1,0:T(8,128)(2,1)} %bitcast.12, bf16[256,2048]{1,0:T(8,128)(2,1)} %shard_map.80.refs_1_, bf16[256,2048]{1,0:T(8,128)(2,1)} %collective-permute-done.15.refs_2_, bf16[256,2048]{1,0:T(8,128)(2,1)} %collective-permute-done.16.refs_3_, ...), custom_call_target="tpu_custom_call" | custom-call | flops 1073741824 | bytes 4194304 | tf_op jit(solution)/shard_map/pallas_call | solution.py:106
  132.3 3.8 %collective-permute-start.11 = (bf16[2,32,1024]{2,1,0:T(8,128)(2,1)S(1)}, bf16[2,32,1024]{2,1,0:T(8,128)(2,1)S(1)}, u32[]{:S(2)}, u32[]{:S(2)}) collective-permute-start(bf16[2,32,1024]{2,1,0:T(8,128)(2,1)S(1)} %get-tuple-element.25), channel_id=1, source_target_pairs={{0,3},{1,0},{2,1},{3,2},{4,7},{5,4},{6,5},{7,6},{8,11},{9,8},{10,9... | collective-permute-start | bytes 393224 | tf_op jit(solution)/shard_map/ppermute | solution.py:46
  136.0 3.0 %collective-permute-done.11 = bf16[2,32,1024]{2,1,0:T(8,128)(2,1)S(1)} collective-permute-done((bf16[2,32,1024]{2,1,0:T(8,128)(2,1)S(1)}, bf16[2,32,1024]{2,1,0:T(8,128)(2,1)S(1)}, u32[]{:S(2)}, u32[]{:S(2)}) %collective-permute-start.11) | collective-permute-done | bytes 131104 | tf_op jit(solution)/shard_map/ppermute | solution.py:46
  139.5 5.4 %collective-permute-done.10 = bf16[2,32,1024]{2,1,0:T(8,128)(2,1)S(1)} collective-permute-done((bf16[2,32,1024]{2,1,0:T(8,128)(2,1)S(1)}, bf16[2,32,1024]{2,1,0:T(8,128)(2,1)S(1)}, u32[]{:S(2)}, u32[]{:S(2)}) %collective-permute-start.10) | collective-permute-done | bytes 131104 | tf_op jit(solution)/shard_map/ppermute | solution.py:46
  145.0 1.7 %convert_add_fusion = f32[2,32,1024]{2,1,0:T(8,128)} fusion(bf16[2,32,1024]{2,1,0:T(8,128)(2,1)S(1)} %collective-permute-done.11, bf16[2,32,1024]{2,1,0:T(8,128)(2,1)S(1)} %collective-permute-done.10, bf16[2,32,1024]{2,1,0:T(8,128)(2,1)S(1)} %collective-permute-done.9, f32[2,128,1024]{2,1,0:T(8,128)} %bitcast.18, s32[]{:T(128)S(6)} %select_n.115), kind=kLoop, calls=%fused_computation.8 | loop fusion | flops 393216 | bytes 917508 | tf_op jit(solution)/shard_map/add | solution.py:47
  147.5 2.2 %shard_map.85.refs_2_ = f32[128,8192]{1,0:T(8,128)} custom-call(f32[128,2048]{1,0:T(8,128)} %get-tuple-element.20.refs_0_, bf16[128,2048]{1,0:T(8,128)(2,1)} %copy-done.10), custom_call_target="tpu_custom_call" | custom-call | flops 524288 | bytes 2621440 | tf_op jit(solution)/shard_map/pallas_call | solution.py:147
  150.5 2.2 %shard_map.86.refs_2_ = f32[128,8192]{1,0:T(8,128)} custom-call(f32[128,2048]{1,0:T(8,128)} %get-tuple-element.18.refs_0_, bf16[128,2048]{1,0:T(8,128)(2,1)} %copy-done.9, f32[128,8192]{1,0:T(8,128)} %shard_map.85.refs_2_), custom_call_target="tpu_custom_call", output_to_operand_aliasing={{}: (2, {})} | custom-call | flops 524288 | bytes 2621440 | tf_op jit(solution)/shard_map/pallas_call | solution.py:147
  153.5 2.2 %shard_map.87.refs_2_ = f32[128,8192]{1,0:T(8,128)} custom-call(f32[128,2048]{1,0:T(8,128)} %get-tuple-element.16.refs_0_, bf16[128,2048]{1,0:T(8,128)(2,1)} %copy-done.7, f32[128,8192]{1,0:T(8,128)} %shard_map.86.refs_2_), custom_call_target="tpu_custom_call", output_to_operand_aliasing={{}: (2, {})} | custom-call | flops 524288 | bytes 2621440 | tf_op jit(solution)/shard_map/pallas_call | solution.py:147
  156.5 2.2 %shard_map.88 = f32[128,8192]{1,0:T(8,128)} custom-call(f32[128,2048]{1,0:T(8,128)} %get-tuple-element.14.refs_0_, bf16[128,2048]{1,0:T(8,128)(2,1)} %copy-done.8, f32[128,8192]{1,0:T(8,128)} %shard_map.87.refs_2_), custom_call_target="tpu_custom_call", output_to_operand_aliasing={{}: (2, {})} | custom-call | flops 524288 | bytes 2621440 | tf_op jit(solution)/shard_map/pallas_call | solution.py:147
  (96 shorter events, 20.9 us)
Async XLA Ops:
  0.6 19.5 %collective-permute-start.6 = (bf16[2,32,1024]{2,1,0:T(8,128)(2,1)}, bf16[2,32,1024]{2,1,0:T(8,128)(2,1)S(1)}, u32[]{:S(2)}, u32[]{:S(2)}) collective-permute-start(bf16[2,32,1024]{2,1,0:T(8,128)(2,1)} %param.7), channel_id=1, source_target_pairs={{0,1},{1,2},{2,3},{3,0},{4,5},{5,6},{6,7},{7,4},{8,9},{9,10},{10,1... | collective-permute-start | bytes 393224 | tf_op jit(solution)/shard_map/ppermute | solution.py:26
  3.7 16.5 %collective-permute-start.8 = (bf16[2,32,1024]{2,1,0:T(8,128)(2,1)}, bf16[2,32,1024]{2,1,0:T(8,128)(2,1)S(1)}, u32[]{:S(2)}, u32[]{:S(2)}) collective-permute-start(bf16[2,32,1024]{2,1,0:T(8,128)(2,1)} %param.7), channel_id=1, source_target_pairs={{0,3},{1,0},{2,1},{3,2},{4,7},{5,4},{6,5},{7,6},{8,11},{9,8},{10,9... | collective-permute-start | bytes 393224 | tf_op jit(solution)/shard_map/ppermute | solution.py:26
  5.8 14.4 %collective-permute-start.7 = (bf16[2,32,1024]{2,1,0:T(8,128)(2,1)}, bf16[2,32,1024]{2,1,0:T(8,128)(2,1)S(1)}, u32[]{:S(2)}, u32[]{:S(2)}) collective-permute-start(bf16[2,32,1024]{2,1,0:T(8,128)(2,1)} %param.7), channel_id=1, source_target_pairs={{0,2},{1,3},{2,0},{3,1},{4,6},{5,7},{6,4},{7,5},{8,10},{9,11},{10,... | collective-permute-start | bytes 393224 | tf_op jit(solution)/shard_map/ppermute | solution.py:26
  7.7 4.2 %collective-permute-start.1 = (bf16[2,32,256]{2,1,0:T(8,128)(2,1)S(1)}, bf16[2,32,256]{2,1,0:T(8,128)(2,1)S(1)}, u32[]{:S(2)}, u32[]{:S(2)}) collective-permute-start(bf16[2,32,256]{2,1,0:T(8,128)(2,1)S(1)} %pad_maximum_fusion.2), channel_id=1, source_target_pairs={{0,8},{4,12},{8,0},{12,4},{16,24},{20,28},{24,16},{28,20},{1,9},{5... | collective-permute-start | bytes 98312 | tf_op jit(solution)/shard_map/ppermute | solution.py:15
  9.3 1.9 %collective-permute-start = (bf16[2,32,256]{2,1,0:T(8,128)(2,1)S(1)}, bf16[2,32,256]{2,1,0:T(8,128)(2,1)S(1)}, u32[]{:S(2)}, u32[]{:S(2)}) collective-permute-start(bf16[2,32,256]{2,1,0:T(8,128)(2,1)S(1)} %get-tuple-element.39), channel_id=1, source_target_pairs={{0,4},{4,0},{8,12},{12,8},{16,20},{20,16},{24,28},{28,24},{1,5},{5... | collective-permute-start | bytes 98312 | tf_op jit(solution)/shard_map/ppermute | solution.py:15
  11.2 3.4 %collective-permute-start.2 = (bf16[2,32,256]{2,1,0:T(8,128)(2,1)S(1)}, bf16[2,32,256]{2,1,0:T(8,128)(2,1)S(1)}, u32[]{:S(2)}, u32[]{:S(2)}) collective-permute-start(bf16[2,32,256]{2,1,0:T(8,128)(2,1)S(1)} %pad_maximum_fusion.3), channel_id=1, source_target_pairs={{0,12},{4,8},{8,4},{12,0},{16,28},{20,24},{24,20},{28,16},{1,13},{... | collective-permute-start | bytes 98312 | tf_op jit(solution)/shard_map/ppermute | solution.py:15
  11.8 8.3 %collective-permute-start.5 = (bf16[2,32,256]{2,1,0:T(8,128)(2,1)S(1)}, bf16[2,32,256]{2,1,0:T(8,128)(2,1)S(1)}, u32[]{:S(2)}, u32[]{:S(2)}) collective-permute-start(bf16[2,32,256]{2,1,0:T(8,128)(2,1)S(1)} %pad_maximum_fusion.5), channel_id=1, source_target_pairs={{0,20},{4,16},{8,28},{12,24},{16,4},{20,0},{24,12},{28,8},{1,21},{... | collective-permute-start | bytes 98312 | tf_op jit(solution)/shard_map/ppermute | solution.py:15
  14.6 1.6 %collective-permute-start.3 = (bf16[2,32,256]{2,1,0:T(8,128)(2,1)S(1)}, bf16[2,32,256]{2,1,0:T(8,128)(2,1)S(1)}, u32[]{:S(2)}, u32[]{:S(2)}) collective-permute-start(bf16[2,32,256]{2,1,0:T(8,128)(2,1)S(1)} %get-tuple-element.38), channel_id=1, source_target_pairs={{0,4},{4,0},{8,12},{12,8},{16,20},{20,16},{24,28},{28,24},{1,5},{5... | collective-permute-start | bytes 98312 | tf_op jit(solution)/shard_map/ppermute | solution.py:15
  16.2 3.9 %collective-permute-start.4 = (bf16[2,32,256]{2,1,0:T(8,128)(2,1)S(1)}, bf16[2,32,256]{2,1,0:T(8,128)(2,1)S(1)}, u32[]{:S(2)}, u32[]{:S(2)}) collective-permute-start(bf16[2,32,256]{2,1,0:T(8,128)(2,1)S(1)} %pad_maximum_fusion.4), channel_id=1, source_target_pairs={{0,16},{4,20},{8,24},{12,28},{16,0},{20,4},{24,8},{28,12},{1,17},{... | collective-permute-start | bytes 98312 | tf_op jit(solution)/shard_map/ppermute | solution.py:15
  26.3 28.7 %collective-permute-start.28 = (bf16[256,2048]{1,0:T(8,128)(2,1)}, bf16[256,2048]{1,0:T(8,128)(2,1)}, u32[]{:S(2)}, u32[]{:S(2)}) collective-permute-start(bf16[256,2048]{1,0:T(8,128)(2,1)} %shard_map.77.refs_1_), channel_id=1, source_target_pairs={{0,8},{4,12},{8,0},{12,4},{16,24},{20,28},{24,16},{28,20},{1,9},{5... | collective-permute-start | bytes 3145736 | tf_op jit(solution)/shard_map/ppermute | solution.py:15
  26.5 29.0 %collective-permute-start.27 = (bf16[256,2048]{1,0:T(8,128)(2,1)}, bf16[256,2048]{1,0:T(8,128)(2,1)}, u32[]{:S(2)}, u32[]{:S(2)}) collective-permute-start(bf16[256,2048]{1,0:T(8,128)(2,1)} %shard_map.77.refs_1_), channel_id=1, source_target_pairs={{0,4},{4,0},{8,12},{12,8},{16,20},{20,16},{24,28},{28,24},{1,5},{5... | collective-permute-start | bytes 3145736 | tf_op jit(solution)/shard_map/ppermute | solution.py:15
  26.5 20.0 %collective-permute-start.14 = (bf16[2,32,2048]{2,1,0:T(8,128)(2,1)S(1)}, bf16[2,32,2048]{2,1,0:T(8,128)(2,1)}, u32[]{:S(2)}, u32[]{:S(2)}) collective-permute-start(bf16[2,32,2048]{2,1,0:T(8,128)(2,1)S(1)} %constant_dynamic-update-slice_fusion), channel_id=1, source_target_pairs={{0,3},{1,0},{2,1},{3,2},{4,7},{5,4},{6,5},{7,6},{8,11},{9,8},{10,9... | collective-permute-start | bytes 786440 | tf_op jit(solution)/shard_map/ppermute | solution.py:26
  27.8 25.5 %collective-permute-start.13 = (bf16[2,32,2048]{2,1,0:T(8,128)(2,1)S(1)}, bf16[2,32,2048]{2,1,0:T(8,128)(2,1)}, u32[]{:S(2)}, u32[]{:S(2)}) collective-permute-start(bf16[2,32,2048]{2,1,0:T(8,128)(2,1)S(1)} %constant_dynamic-update-slice_fusion), channel_id=1, source_target_pairs={{0,2},{1,3},{2,0},{3,1},{4,6},{5,7},{6,4},{7,5},{8,10},{9,11},{10,... | collective-permute-start | bytes 786440 | tf_op jit(solution)/shard_map/ppermute | solution.py:26
  29.7 23.7 %collective-permute-start.12 = (bf16[2,32,2048]{2,1,0:T(8,128)(2,1)S(1)}, bf16[2,32,2048]{2,1,0:T(8,128)(2,1)}, u32[]{:S(2)}, u32[]{:S(2)}) collective-permute-start(bf16[2,32,2048]{2,1,0:T(8,128)(2,1)S(1)} %constant_dynamic-update-slice_fusion), channel_id=1, source_target_pairs={{0,1},{1,2},{2,3},{3,0},{4,5},{5,6},{6,7},{7,4},{8,9},{9,10},{10,1... | collective-permute-start | bytes 786440 | tf_op jit(solution)/shard_map/ppermute | solution.py:26
  46.5 26.8 %collective-permute-start.20 = (bf16[256,2048]{1,0:T(8,128)(2,1)}, bf16[256,2048]{1,0:T(8,128)(2,1)}, u32[]{:S(2)}, u32[]{:S(2)}) collective-permute-start(bf16[256,2048]{1,0:T(8,128)(2,1)} %shard_map.78.refs_1_), channel_id=1, source_target_pairs={{0,8},{4,12},{8,0},{12,4},{16,24},{20,28},{24,16},{28,20},{1,9},{5... | collective-permute-start | bytes 3145736 | tf_op jit(solution)/shard_map/ppermute | solution.py:15
  53.3 20.0 %collective-permute-start.19 = (bf16[256,2048]{1,0:T(8,128)(2,1)}, bf16[256,2048]{1,0:T(8,128)(2,1)S(1)}, u32[]{:S(2)}, u32[]{:S(2)}) collective-permute-start(bf16[256,2048]{1,0:T(8,128)(2,1)} %shard_map.78.refs_1_), channel_id=1, source_target_pairs={{0,4},{4,0},{8,12},{12,8},{16,20},{20,16},{24,28},{28,24},{1,5},{5... | collective-permute-start | bytes 3145736 | tf_op jit(solution)/shard_map/ppermute | solution.py:15
  53.3 26.2 %collective-permute-start.24 = (bf16[256,2048]{1,0:T(8,128)(2,1)S(1)}, bf16[256,2048]{1,0:T(8,128)(2,1)}, u32[]{:S(2)}, u32[]{:S(2)}) collective-permute-start(bf16[256,2048]{1,0:T(8,128)(2,1)S(1)} %copy-done.3), channel_id=1, source_target_pairs={{0,16},{4,20},{8,24},{12,28},{16,0},{20,4},{24,8},{28,12},{1,17},{... | collective-permute-start | bytes 3145736 | tf_op jit(solution)/shard_map/ppermute | solution.py:15
  54.9 46.6 %collective-permute-start.16 = (bf16[256,2048]{1,0:T(8,128)(2,1)S(1)}, bf16[256,2048]{1,0:T(8,128)(2,1)}, u32[]{:S(2)}, u32[]{:S(2)}) collective-permute-start(bf16[256,2048]{1,0:T(8,128)(2,1)S(1)} %copy-done.2), channel_id=1, source_target_pairs={{0,16},{4,20},{8,24},{12,28},{16,0},{20,4},{24,8},{28,12},{1,17},{... | collective-permute-start | bytes 3145736 | tf_op jit(solution)/shard_map/ppermute | solution.py:15
  55.5 46.0 %collective-permute-start.29 = (bf16[256,2048]{1,0:T(8,128)(2,1)}, bf16[256,2048]{1,0:T(8,128)(2,1)S(1)}, u32[]{:S(2)}, u32[]{:S(2)}) collective-permute-start(bf16[256,2048]{1,0:T(8,128)(2,1)} %collective-permute-done.28.refs_3_), channel_id=1, source_target_pairs={{0,4},{4,0},{8,12},{12,8},{16,20},{20,16},{24,28},{28,24},{1,5},{5... | collective-permute-start | bytes 3145736 | tf_op jit(solution)/shard_map/ppermute | solution.py:15
  66.1 38.9 %copy-start.11 = (f32[256,1024]{1,0:T(8,128)}, f32[256,1024]{1,0:T(8,128)S(1)}, u32[]{:S(2)}) copy-start(f32[256,1024]{1,0:T(8,128)S(1)} %fusion) | copy-start | bytes 3145732
  73.3 43.9 %collective-permute-start.23 = (bf16[256,2048]{1,0:T(8,128)(2,1)S(1)}, bf16[256,2048]{1,0:T(8,128)(2,1)}, u32[]{:S(2)}, u32[]{:S(2)}) collective-permute-start(bf16[256,2048]{1,0:T(8,128)(2,1)S(1)} %copy-done.3), channel_id=1, source_target_pairs={{0,4},{4,0},{8,12},{12,8},{16,20},{20,16},{24,28},{28,24},{1,5},{5... | collective-permute-start | bytes 3145736 | tf_op jit(solution)/shard_map/ppermute | solution.py:15
  73.3 38.2 %collective-permute-start.21 = (bf16[256,2048]{1,0:T(8,128)(2,1)}, bf16[256,2048]{1,0:T(8,128)(2,1)}, u32[]{:S(2)}, u32[]{:S(2)}) collective-permute-start(bf16[256,2048]{1,0:T(8,128)(2,1)} %collective-permute-done.20.refs_3_), channel_id=1, source_target_pairs={{0,4},{4,0},{8,12},{12,8},{16,20},{20,16},{24,28},{28,24},{1,5},{5... | collective-permute-start | bytes 3145736 | tf_op jit(solution)/shard_map/ppermute | solution.py:15
  79.6 39.3 %collective-permute-start.25 = (bf16[256,2048]{1,0:T(8,128)(2,1)}, bf16[256,2048]{1,0:T(8,128)(2,1)}, u32[]{:S(2)}, u32[]{:S(2)}) collective-permute-start(bf16[256,2048]{1,0:T(8,128)(2,1)} %collective-permute-done.24.refs_3_), channel_id=1, source_target_pairs={{0,4},{4,0},{8,12},{12,8},{16,20},{20,16},{24,28},{28,24},{1,5},{5... | collective-permute-start | bytes 3145736 | tf_op jit(solution)/shard_map/ppermute | solution.py:15
  101.5 23.2 %collective-permute-start.15 = (bf16[256,2048]{1,0:T(8,128)(2,1)S(1)}, bf16[256,2048]{1,0:T(8,128)(2,1)}, u32[]{:S(2)}, u32[]{:S(2)}) collective-permute-start(bf16[256,2048]{1,0:T(8,128)(2,1)S(1)} %copy-done.2), channel_id=1, source_target_pairs={{0,4},{4,0},{8,12},{12,8},{16,20},{20,16},{24,28},{28,24},{1,5},{5... | collective-permute-start | bytes 3145736 | tf_op jit(solution)/shard_map/ppermute | solution.py:15
  101.5 25.0 %collective-permute-start.17 = (bf16[256,2048]{1,0:T(8,128)(2,1)}, bf16[256,2048]{1,0:T(8,128)(2,1)}, u32[]{:S(2)}, u32[]{:S(2)}) collective-permute-start(bf16[256,2048]{1,0:T(8,128)(2,1)} %collective-permute-done.16.refs_3_), channel_id=1, source_target_pairs={{0,4},{4,0},{8,12},{12,8},{16,20},{20,16},{24,28},{28,24},{1,5},{5... | collective-permute-start | bytes 3145736 | tf_op jit(solution)/shard_map/ppermute | solution.py:15
  111.5 20.7 %collective-permute-start.9 = (bf16[2,32,1024]{2,1,0:T(8,128)(2,1)S(1)}, bf16[2,32,1024]{2,1,0:T(8,128)(2,1)S(1)}, u32[]{:S(2)}, u32[]{:S(2)}) collective-permute-start(bf16[2,32,1024]{2,1,0:T(8,128)(2,1)S(1)} %get-tuple-element.24), channel_id=1, source_target_pairs={{0,1},{1,2},{2,3},{3,0},{4,5},{5,6},{6,7},{7,4},{8,9},{9,10},{10,1... | collective-permute-start | bytes 393224 | tf_op jit(solution)/shard_map/ppermute | solution.py:46
  117.2 29.5 %collective-permute-start.30 = (bf16[128,2048]{1,0:T(8,128)(2,1)S(1)}, bf16[128,2048]{1,0:T(8,128)(2,1)S(1)}, u32[]{:S(2)}, u32[]{:S(2)}) collective-permute-start(bf16[128,2048]{1,0:T(8,128)(2,1)S(1)} %copy-done.12), channel_id=1, source_target_pairs={{0,16},{4,20},{8,24},{12,28},{16,0},{20,4},{24,8},{28,12},{1,17},{... | collective-permute-start | bytes 1572872 | tf_op jit(solution)/shard_map/ppermute | solution.py:15
  118.8 33.9 %collective-permute-start.22 = (bf16[128,2048]{1,0:T(8,128)(2,1)}, bf16[128,2048]{1,0:T(8,128)(2,1)S(1)}, u32[]{:S(2)}, u32[]{:S(2)}) collective-permute-start(bf16[128,2048]{1,0:T(8,128)(2,1)} %get-tuple-element.17), channel_id=1, source_target_pairs={{0,16},{4,20},{8,24},{12,28},{16,0},{20,4},{24,8},{28,12},{1,17},{... | collective-permute-start | bytes 1572872 | tf_op jit(solution)/shard_map/ppermute | solution.py:15
  124.7 24.9 %collective-permute-start.26 = (bf16[128,2048]{1,0:T(8,128)(2,1)}, bf16[128,2048]{1,0:T(8,128)(2,1)S(1)}, u32[]{:S(2)}, u32[]{:S(2)}) collective-permute-start(bf16[128,2048]{1,0:T(8,128)(2,1)} %get-tuple-element.19), channel_id=1, source_target_pairs={{0,8},{4,12},{8,0},{12,4},{16,24},{20,28},{24,16},{28,20},{1,9},{5... | collective-permute-start | bytes 1572872 | tf_op jit(solution)/shard_map/ppermute | solution.py:15
  131.9 23.8 %collective-permute-start.18 = (bf16[128,2048]{1,0:T(8,128)(2,1)}, bf16[128,2048]{1,0:T(8,128)(2,1)S(1)}, u32[]{:S(2)}, u32[]{:S(2)}) collective-permute-start(bf16[128,2048]{1,0:T(8,128)(2,1)} %get-tuple-element.15), channel_id=1, source_target_pairs={{0,8},{4,12},{8,0},{12,4},{16,24},{20,28},{24,16},{28,20},{1,9},{5... | collective-permute-start | bytes 1572872 | tf_op jit(solution)/shard_map/ppermute | solution.py:15
  132.3 6.8 %collective-permute-start.11 = (bf16[2,32,1024]{2,1,0:T(8,128)(2,1)S(1)}, bf16[2,32,1024]{2,1,0:T(8,128)(2,1)S(1)}, u32[]{:S(2)}, u32[]{:S(2)}) collective-permute-start(bf16[2,32,1024]{2,1,0:T(8,128)(2,1)S(1)} %get-tuple-element.25), channel_id=1, source_target_pairs={{0,3},{1,0},{2,1},{3,2},{4,7},{5,4},{6,5},{7,6},{8,11},{9,8},{10,9... | collective-permute-start | bytes 393224 | tf_op jit(solution)/shard_map/ppermute | solution.py:46
  139.1 5.9 %collective-permute-start.10 = (bf16[2,32,1024]{2,1,0:T(8,128)(2,1)S(1)}, bf16[2,32,1024]{2,1,0:T(8,128)(2,1)S(1)}, u32[]{:S(2)}, u32[]{:S(2)}) collective-permute-start(bf16[2,32,1024]{2,1,0:T(8,128)(2,1)S(1)} %get-tuple-element.26), channel_id=1, source_target_pairs={{0,2},{1,3},{2,0},{3,1},{4,6},{5,7},{6,4},{7,5},{8,10},{9,11},{10,... | collective-permute-start | bytes 393224 | tf_op jit(solution)/shard_map/ppermute | solution.py:46
  (12 other events, 86.1 us)
